TPU v7x, 768 devices: a whole 4x8x12 slice. The times are simulated.
768 devices in a mesh: lon: 32 (over y, x_lo, core), lat: 24 (over z, x_hi).
Axes of the slice: x: 4 (x_hi: 2, x_lo: 2; x = x_hi * 2 + x_lo), y: 8, z: 12, core: 2. Of those that a mesh axis runs over, the one named last changes fastest.
Arguments:
- velocity: float32 [2, 1536, 8192], P(None, 'lat', 'lon'), may hold values from -4 to 4
- stress: float32 [3, 1536, 8192], P(None, 'lat', 'lon'), may hold values from -4 to 4
- thickness: float32 [6, 1536, 8192], P(None, 'lat', 'lon'), may hold values from 0.1 to 5
- concentration: float32 [6, 1536, 8192], P(None, 'lat', 'lon'), may hold values from 0.02 to 0.16
- land_mask: int32 [1536, 8192], P('lat', 'lon'), may hold values 0 or 1
- covered: int32 [24, 64], P('lat'), may hold values 0 or 1
- ocean_current: bfloat16 [2, 2, 1536, 8192], P(None, None, 'lat', 'lon'), may hold values from -6 to 6
- wind_stress: bfloat16 [2, 2, 1536, 8192], P(None, None, 'lat', 'lon'), may hold values from -6 to 6
- regrid_weights: bfloat16 [1536, 128], P('lat'), may hold values from -0.5 to 0.5
- tile_offset: int32 [1536], P('lat'), may hold values from -1 to 1, as said below
Outputs:
- velocity_out: float32 [2, 1536, 8192], P(None, 'lat', 'lon')
- stress_out: float32 [3, 1536, 8192], P(None, 'lat', 'lon')
- thickness_out: float32 [6, 1536, 8192], P(None, 'lat', 'lon')
Inputs may be any that keep to these rules, and one draw needn't show every extreme that they name: `tile_offset`: never 0; rows of the first tile have +1 and rows of the last tile have -1, so every row reads a tile of the grid.
All inputs are finite; a program needn't handle non-finite values. No bound on the sum of `land_mask` or of `covered` on one device may be relied on, other than what follows from the above.
Results may differ from a plain program's by a relative error of at most 0.0015.
Values may be sent and summed in bfloat16 or wider, within the bound.
A program may use at most 32 MiB of HBM per device.

v0:
```python
import jax
import jax.numpy as jnp
from jax import lax
from jax.sharding import PartitionSpec as P

BPD = 2
SUB = 4


relax_rate = 0.5
strain_offset = 0.5
time_step = 0.5
water_drag = 1.0
growth_rate = 0.3
mixing_rate = 0.3


def padded(x, sides, width, wrap):
    for axis, dim in sides:
        devices, length = (lax.axis_size(axis), x.shape[dim])
        up = [(i, (i + 1) % devices) for i in range(devices if wrap else devices - 1)]
        down = [(j, i) for i, j in up]
        last = lax.slice_in_dim(x, length - width, length, axis=dim)
        leading = lax.slice_in_dim(x, 0, width, axis=dim)
        before = lax.ppermute(last, axis, up)
        after = lax.ppermute(leading, axis, down)
        x = jnp.concatenate([before, x, after], axis=dim)
    return x


def growth(thick_now, conc_now):
    ice_area = jnp.sum(conc_now, axis=0)
    mean_thick = jnp.sum(conc_now * thick_now, axis=0) / ice_area
    return thick_now + growth_rate / (0.5 + thick_now) + mixing_rate * (mean_thick - thick_now)


def keep_thick(thick_now, conc_now):
    return thick_now


def grow_block(thick_block, conc_block, live):
    return lax.cond(live, growth, keep_thick, thick_block, conc_block)


def forcing(thick_now, conc_now):
    volume = jnp.sum(conc_now * thick_now, axis=0)
    ice_area = jnp.sum(conc_now, axis=0)
    strength = volume * jnp.exp(-2.0 * (1.0 - ice_area))
    return (strength, volume + 0.5)


def new_stress(
    east_u,
    west_u,
    north_u,
    south_u,
    east_v,
    west_v,
    north_v,
    south_v,
    stresses,
    strength,
    open_mask,
):
    stretch_x = (east_u - west_u) / 2.0
    stretch_y = (north_v - south_v) / 2.0
    shear_half = (north_u - south_u + (east_v - west_v)) / 4.0
    divergence = stretch_x + stretch_y
    tension = stretch_x - stretch_y
    shearing = 2.0 * shear_half
    deformation = jnp.sqrt(
        divergence * divergence
        + (tension * tension + shearing * shearing) / 4.0
        + strain_offset * strain_offset
    )
    bulk_stress = (
        (stresses[0] + relax_rate * strength * (divergence / deformation - 1.0))
        / (1.0 + relax_rate)
        * open_mask
    )
    tension_stress = (
        (stresses[1] + relax_rate * strength * tension / (4.0 * deformation))
        / (1.0 + relax_rate)
        * open_mask
    )
    shear_stress = (
        (stresses[2] + relax_rate * strength * shearing / (8.0 * deformation))
        / (1.0 + relax_rate)
        * open_mask
    )
    return jnp.stack([bulk_stress, tension_stress, shear_stress])


def new_velocity(
    sxx_east,
    sxx_west,
    syy_north,
    syy_south,
    sxy_east,
    sxy_west,
    sxy_north,
    sxy_south,
    velocity_now,
    ice_mass,
    current,
    wind_now,
    open_mask,
):
    force_x = (sxx_east - sxx_west) / 2.0 + (sxy_north - sxy_south) / 2.0
    force_y = (sxy_east - sxy_west) / 2.0 + (syy_north - syy_south) / 2.0
    damping = 1.0 + time_step * water_drag / ice_mass
    u = (
        (velocity_now[0] + time_step * (force_x + wind_now[0] + water_drag * current[0]) / ice_mass)
        / damping
        * open_mask
    )
    v = (
        (velocity_now[1] + time_step * (force_y + wind_now[1] + water_drag * current[1]) / ice_mass)
        / damping
        * open_mask
    )
    return jnp.stack([u, v])


def stress_from(wide_velocity, stresses, strength, open_mask):
    u = wide_velocity[0]
    v = wide_velocity[1]
    return new_stress(
        u[1:-1, 2:],
        u[1:-1, :-2],
        u[2:, 1:-1],
        u[:-2, 1:-1],
        v[1:-1, 2:],
        v[1:-1, :-2],
        v[2:, 1:-1],
        v[:-2, 1:-1],
        stresses,
        strength,
        open_mask,
    )


def velocity_from(wide_stress, velocity_now, ice_mass, current, wind_now, open_mask):
    sigma_xx = (wide_stress[0] + wide_stress[1]) / 2.0
    sigma_yy = (wide_stress[0] - wide_stress[1]) / 2.0
    sigma_xy = wide_stress[2]
    return new_velocity(
        sigma_xx[1:-1, 2:],
        sigma_xx[1:-1, :-2],
        sigma_yy[2:, 1:-1],
        sigma_yy[:-2, 1:-1],
        sigma_xy[1:-1, 2:],
        sigma_xy[1:-1, :-2],
        sigma_xy[2:, 1:-1],
        sigma_xy[:-2, 1:-1],
        velocity_now,
        ice_mass,
        current,
        wind_now,
        open_mask,
    )


def local(
    velocity,
    stress,
    thickness,
    concentration,
    land_mask,
    covered,
    ocean_current,
    wind_stress,
    regrid_weights,
    tile_offset,
):
    row_count = velocity.shape[1]
    col_count = velocity.shape[2]
    blocks = BPD
    block_cols = col_count // blocks
    lon_pos = lax.axis_index("lon")
    lat_count = lax.axis_size("lat")
    lat_pos = lax.axis_index("lat")
    open_mask = land_mask.astype(jnp.float32)

    def inside_rows(total_rows, margin):
        numbers = jnp.arange(total_rows)[:, None]
        outside = (numbers < margin) & (lat_pos == 0) | (numbers >= total_rows - margin) & (
            lat_pos == lat_count - 1
        )
        return jnp.where(outside, 0.0, 1.0).astype(jnp.float32)

    beside_all = padded(ocean_current, (("lat", 2),), row_count, False)
    side_weights = regrid_weights[:, row_count:]
    currents = jnp.einsum(
        "ij,wcjx->wcix",
        regrid_weights[:, :row_count],
        ocean_current,
        preferred_element_type=jnp.float32,
    )
    from_lower = jnp.einsum(
        "ij,wcjx->wcix",
        side_weights,
        beside_all[:, :, :row_count],
        preferred_element_type=jnp.float32,
    )
    from_upper = jnp.einsum(
        "ij,wcjx->wcix",
        side_weights,
        beside_all[:, :, 2 * row_count :],
        preferred_element_type=jnp.float32,
    )
    upward = (tile_offset > 0)[:, None]
    currents = currents + jnp.where(upward, from_upper, from_lower)
    own_flags = lax.dynamic_slice_in_dim(covered[0], lon_pos * blocks, blocks)

    def extend(fields):
        wide = padded(fields.astype(jnp.bfloat16), (("lon", 2), ("lat", 1)), 1, True).astype(
            fields.dtype
        )
        return wide * inside_rows(row_count + 2, 1)

    thick_now = thickness
    velocity_now = velocity
    stresses = stress
    for window in range(wind_stress.shape[0]):
        pieces = []
        for number in range(blocks):
            columns = slice(number * block_cols, (number + 1) * block_cols)
            pieces.append(
                grow_block(
                    thick_now[:, :, columns], concentration[:, :, columns], own_flags[number] > 0
                )
            )
        thick_now = jnp.concatenate(pieces, axis=2)
        strength, ice_mass = forcing(thick_now, concentration)
        wind_now = wind_stress[window].astype(jnp.float32)
        current = currents[window]
        for substep in range(SUB):
            stresses = stress_from(extend(velocity_now), stresses, strength, open_mask)
            velocity_now = velocity_from(
                extend(stresses), velocity_now, ice_mass, current, wind_now, open_mask
            )
    return (velocity_now, stresses, thick_now)


def solution(mesh):
    return jax.shard_map(
        local,
        mesh=mesh,
        in_specs=(
            P(None, "lat", "lon"),
            P(None, "lat", "lon"),
            P(None, "lat", "lon"),
            P(None, "lat", "lon"),
            P("lat", "lon"),
            P("lat", None),
            P(None, None, "lat", "lon"),
            P(None, None, "lat", "lon"),
            P("lat", None),
            P("lat"),
        ),
        out_specs=(P(None, "lat", "lon"), P(None, "lat", "lon"), P(None, "lat", "lon")),
        check_vma=False,
    )
```

profile of v0, /device:TPU:31, one launch (start us, length us, event | category | flops | bytes accessed | tf_op | source)
XLA Modules:
  0.0 374.9 jit_solution(17116250240514374376)
XLA Ops:
  0.7 5.0 %collective-permute-start.9 = (bf16[2,2,64,256]{3,2,1,0:T(8,128)(2,1)}, bf16[2,2,64,256]{3,2,1,0:T(8,128)(2,1)S(1)}, u32[]{:S(2)}, u32[]{:S(2)}) collective-permute-start(bf16[2,2,64,256]{3,2,1,0:T(8,128)(2,1)} %param.24), channel_id=1, source_target_pairs={{0,1},{1,2},{2,3},{3,4},{4,5},{5,6},{6,7},{7,8},{8,9},{9,10},{10,1... | collective-permute-start | bytes 393224 | tf_op jit(solution)/shard_map/ppermute | solution.py:25
  8.6 5.8 %collective-permute-start = (bf16[2,64,1]{2,1,0:T(8,128)(2,1)S(1)}, bf16[2,64,1]{2,1,0:T(8,128)(2,1)S(1)}, u32[]{:S(2)}, u32[]{:S(2)}) collective-permute-start(bf16[2,64,1]{2,1,0:T(8,128)(2,1)S(1)} %get-tuple-element.294), channel_id=1, source_target_pairs={{0,24},{24,48},{48,72},{72,96},{96,120},{120,144},{144,168},{168,1... | collective-permute-start | bytes 776 | tf_op jit(solution)/shard_map/ppermute | solution.py:25
  22.2 5.1 %collective-permute-start.2 = (bf16[2,1,258]{2,1,0:T(2,128)(2,1)S(1)}, bf16[2,1,258]{2,1,0:T(2,128)(2,1)S(1)}, u32[]{:S(2)}, u32[]{:S(2)}) collective-permute-start(bf16[2,1,258]{2,1,0:T(2,128)(2,1)S(1)} %get-tuple-element.262), channel_id=1, source_target_pairs={{0,1},{1,2},{2,3},{3,4},{4,5},{5,6},{6,7},{7,8},{8,9},{9,10},{10,1... | collective-permute-start | bytes 3104 | tf_op jit(solution)/shard_map/ppermute | solution.py:25
  35.6 7.0 %collective-permute-start.4 = (bf16[3,64,1]{2,1,0:T(8,128)(2,1)S(1)}, bf16[3,64,1]{2,1,0:T(8,128)(2,1)S(1)}, u32[]{:S(2)}, u32[]{:S(2)}) collective-permute-start(bf16[3,64,1]{2,1,0:T(8,128)(2,1)S(1)} %get-tuple-element.278), channel_id=1, source_target_pairs={{0,24},{24,48},{48,72},{72,96},{96,120},{120,144},{144,168},{168,1... | collective-permute-start | bytes 1160 | tf_op jit(solution)/shard_map/ppermute | solution.py:25
  44.5 5.5 %collective-permute-done.5 = bf16[3,64,1]{2,1,0:T(8,128)(2,1)S(1)} collective-permute-done((bf16[3,64,1]{2,1,0:T(8,128)(2,1)S(1)}, bf16[3,64,1]{2,1,0:T(8,128)(2,1)S(1)}, u32[]{:S(2)}, u32[]{:S(2)}) %collective-permute-start.5) | collective-permute-done | bytes 416 | tf_op jit(solution)/shard_map/ppermute | solution.py:26
  53.3 8.4 %collective-permute-start.7 = (bf16[3,1,258]{2,1,0:T(2,128)(2,1)S(1)}, bf16[3,1,258]{2,1,0:T(2,128)(2,1)S(1)}, u32[]{:S(2)}, u32[]{:S(2)}) collective-permute-start(bf16[3,1,258]{2,1,0:T(2,128)(2,1)S(1)} %get-tuple-element.245), channel_id=1, source_target_pairs={{1,0},{2,1},{3,2},{4,3},{5,4},{6,5},{7,6},{8,7},{9,8},{10,9},{11,1... | collective-permute-start | bytes 4652 | tf_op jit(solution)/shard_map/ppermute | solution.py:26
  68.4 5.1 %collective-permute-done.11 = bf16[2,64,1]{2,1,0:T(8,128)(2,1)S(1)} collective-permute-done((bf16[2,64,1]{2,1,0:T(8,128)(2,1)S(1)}, bf16[2,64,1]{2,1,0:T(8,128)(2,1)S(1)}, u32[]{:S(2)}, u32[]{:S(2)}) %collective-permute-start.11) | collective-permute-done | bytes 288 | tf_op jit(solution)/shard_map/ppermute | solution.py:26
  77.6 6.1 %collective-permute-start.13 = (bf16[2,1,258]{2,1,0:T(2,128)(2,1)S(1)}, bf16[2,1,258]{2,1,0:T(2,128)(2,1)S(1)}, u32[]{:S(2)}, u32[]{:S(2)}) collective-permute-start(bf16[2,1,258]{2,1,0:T(2,128)(2,1)S(1)} %get-tuple-element.261), channel_id=1, source_target_pairs={{1,0},{2,1},{3,2},{4,3},{5,4},{6,5},{7,6},{8,7},{9,8},{10,9},{11,1... | collective-permute-start | bytes 3104 | tf_op jit(solution)/shard_map/ppermute | solution.py:26
  89.6 5.6 %collective-permute-done.15 = bf16[3,64,1]{2,1,0:T(8,128)(2,1)S(1)} collective-permute-done((bf16[3,64,1]{2,1,0:T(8,128)(2,1)S(1)}, bf16[3,64,1]{2,1,0:T(8,128)(2,1)S(1)}, u32[]{:S(2)}, u32[]{:S(2)}) %collective-permute-start.15) | collective-permute-done | bytes 416 | tf_op jit(solution)/shard_map/ppermute | solution.py:26
  98.4 6.5 %collective-permute-start.17 = (bf16[3,1,258]{2,1,0:T(2,128)(2,1)S(1)}, bf16[3,1,258]{2,1,0:T(2,128)(2,1)S(1)}, u32[]{:S(2)}, u32[]{:S(2)}) collective-permute-start(bf16[3,1,258]{2,1,0:T(2,128)(2,1)S(1)} %get-tuple-element.243), channel_id=1, source_target_pairs={{1,0},{2,1},{3,2},{4,3},{5,4},{6,5},{7,6},{8,7},{9,8},{10,9},{11,1... | collective-permute-start | bytes 4652 | tf_op jit(solution)/shard_map/ppermute | solution.py:26
  111.0 5.4 %collective-permute-done.19 = bf16[2,64,1]{2,1,0:T(8,128)(2,1)S(1)} collective-permute-done((bf16[2,64,1]{2,1,0:T(8,128)(2,1)S(1)}, bf16[2,64,1]{2,1,0:T(8,128)(2,1)S(1)}, u32[]{:S(2)}, u32[]{:S(2)}) %collective-permute-start.19) | collective-permute-done | bytes 288 | tf_op jit(solution)/shard_map/ppermute | solution.py:26
  116.5 5.8 %collective-permute-start.20 = (bf16[2,1,258]{2,1,0:T(2,128)(2,1)S(1)}, bf16[2,1,258]{2,1,0:T(2,128)(2,1)S(1)}, u32[]{:S(2)}, u32[]{:S(2)}) collective-permute-start(bf16[2,1,258]{2,1,0:T(2,128)(2,1)S(1)} %get-tuple-element.258), channel_id=1, source_target_pairs={{0,1},{1,2},{2,3},{3,4},{4,5},{5,6},{6,7},{7,8},{8,9},{9,10},{10,1... | collective-permute-start | bytes 3104 | tf_op jit(solution)/shard_map/ppermute | solution.py:25
  134.2 5.6 %collective-permute-done.23 = bf16[3,64,1]{2,1,0:T(8,128)(2,1)S(1)} collective-permute-done((bf16[3,64,1]{2,1,0:T(8,128)(2,1)S(1)}, bf16[3,64,1]{2,1,0:T(8,128)(2,1)S(1)}, u32[]{:S(2)}, u32[]{:S(2)}) %collective-permute-start.23) | collective-permute-done | bytes 416 | tf_op jit(solution)/shard_map/ppermute | solution.py:26
  139.9 5.8 %collective-permute-start.24 = (bf16[3,1,258]{2,1,0:T(2,128)(2,1)S(1)}, bf16[3,1,258]{2,1,0:T(2,128)(2,1)S(1)}, u32[]{:S(2)}, u32[]{:S(2)}) collective-permute-start(bf16[3,1,258]{2,1,0:T(2,128)(2,1)S(1)} %get-tuple-element.240), channel_id=1, source_target_pairs={{0,1},{1,2},{2,3},{3,4},{4,5},{5,6},{6,7},{7,8},{8,9},{9,10},{10,1... | collective-permute-start | bytes 4652 | tf_op jit(solution)/shard_map/ppermute | solution.py:25
  147.7 4.8 %collective-permute-done.25 = bf16[3,1,258]{2,1,0:T(2,128)(2,1)S(1)} collective-permute-done((bf16[3,1,258]{2,1,0:T(2,128)(2,1)S(1)}, bf16[3,1,258]{2,1,0:T(2,128)(2,1)S(1)}, u32[]{:S(2)}, u32[]{:S(2)}) %collective-permute-start.25) | collective-permute-done | bytes 1580 | tf_op jit(solution)/shard_map/ppermute | solution.py:26
  157.6 5.4 %collective-permute-done.27 = bf16[2,64,1]{2,1,0:T(8,128)(2,1)S(1)} collective-permute-done((bf16[2,64,1]{2,1,0:T(8,128)(2,1)S(1)}, bf16[2,64,1]{2,1,0:T(8,128)(2,1)S(1)}, u32[]{:S(2)}, u32[]{:S(2)}) %collective-permute-start.27) | collective-permute-done | bytes 288 | tf_op jit(solution)/shard_map/ppermute | solution.py:26
  163.1 5.8 %collective-permute-start.28 = (bf16[2,1,258]{2,1,0:T(2,128)(2,1)S(1)}, bf16[2,1,258]{2,1,0:T(2,128)(2,1)S(1)}, u32[]{:S(2)}, u32[]{:S(2)}) collective-permute-start(bf16[2,1,258]{2,1,0:T(2,128)(2,1)S(1)} %get-tuple-element.256), channel_id=1, source_target_pairs={{0,1},{1,2},{2,3},{3,4},{4,5},{5,6},{6,7},{7,8},{8,9},{9,10},{10,1... | collective-permute-start | bytes 3104 | tf_op jit(solution)/shard_map/ppermute | solution.py:25
  170.8 4.8 %collective-permute-done.29 = bf16[2,1,258]{2,1,0:T(2,128)(2,1)S(1)} collective-permute-done((bf16[2,1,258]{2,1,0:T(2,128)(2,1)S(1)}, bf16[2,1,258]{2,1,0:T(2,128)(2,1)S(1)}, u32[]{:S(2)}, u32[]{:S(2)}) %collective-permute-start.29) | collective-permute-done | bytes 1064 | tf_op jit(solution)/shard_map/ppermute | solution.py:26
  180.9 5.6 %collective-permute-done.31 = bf16[3,64,1]{2,1,0:T(8,128)(2,1)S(1)} collective-permute-done((bf16[3,64,1]{2,1,0:T(8,128)(2,1)S(1)}, bf16[3,64,1]{2,1,0:T(8,128)(2,1)S(1)}, u32[]{:S(2)}, u32[]{:S(2)}) %collective-permute-start.31) | collective-permute-done | bytes 416 | tf_op jit(solution)/shard_map/ppermute | solution.py:26
  201.8 5.4 %collective-permute-done.35 = bf16[2,64,1]{2,1,0:T(8,128)(2,1)S(1)} collective-permute-done((bf16[2,64,1]{2,1,0:T(8,128)(2,1)S(1)}, bf16[2,64,1]{2,1,0:T(8,128)(2,1)S(1)}, u32[]{:S(2)}, u32[]{:S(2)}) %collective-permute-start.35) | collective-permute-done | bytes 288 | tf_op jit(solution)/shard_map/ppermute | solution.py:26
  223.7 5.6 %collective-permute-done.39 = bf16[3,64,1]{2,1,0:T(8,128)(2,1)S(1)} collective-permute-done((bf16[3,64,1]{2,1,0:T(8,128)(2,1)S(1)}, bf16[3,64,1]{2,1,0:T(8,128)(2,1)S(1)}, u32[]{:S(2)}, u32[]{:S(2)}) %collective-permute-start.39) | collective-permute-done | bytes 416 | tf_op jit(solution)/shard_map/ppermute | solution.py:26
  244.7 5.4 %collective-permute-done.43 = bf16[2,64,1]{2,1,0:T(8,128)(2,1)S(1)} collective-permute-done((bf16[2,64,1]{2,1,0:T(8,128)(2,1)S(1)}, bf16[2,64,1]{2,1,0:T(8,128)(2,1)S(1)}, u32[]{:S(2)}, u32[]{:S(2)}) %collective-permute-start.43) | collective-permute-done | bytes 288 | tf_op jit(solution)/shard_map/ppermute | solution.py:26
  250.2 5.3 %collective-permute-start.44 = (bf16[2,1,258]{2,1,0:T(2,128)(2,1)S(1)}, bf16[2,1,258]{2,1,0:T(2,128)(2,1)S(1)}, u32[]{:S(2)}, u32[]{:S(2)}) collective-permute-start(bf16[2,1,258]{2,1,0:T(2,128)(2,1)S(1)} %get-tuple-element.250), channel_id=1, source_target_pairs={{0,1},{1,2},{2,3},{3,4},{4,5},{5,6},{6,7},{7,8},{8,9},{9,10},{10,1... | collective-permute-start | bytes 3104 | tf_op jit(solution)/shard_map/ppermute | solution.py:25
  257.5 4.8 %collective-permute-done.45 = bf16[2,1,258]{2,1,0:T(2,128)(2,1)S(1)} collective-permute-done((bf16[2,1,258]{2,1,0:T(2,128)(2,1)S(1)}, bf16[2,1,258]{2,1,0:T(2,128)(2,1)S(1)}, u32[]{:S(2)}, u32[]{:S(2)}) %collective-permute-start.45) | collective-permute-done | bytes 1064 | tf_op jit(solution)/shard_map/ppermute | solution.py:26
  267.5 5.6 %collective-permute-done.47 = bf16[3,64,1]{2,1,0:T(8,128)(2,1)S(1)} collective-permute-done((bf16[3,64,1]{2,1,0:T(8,128)(2,1)S(1)}, bf16[3,64,1]{2,1,0:T(8,128)(2,1)S(1)}, u32[]{:S(2)}, u32[]{:S(2)}) %collective-permute-start.47) | collective-permute-done | bytes 416 | tf_op jit(solution)/shard_map/ppermute | solution.py:26
  288.9 5.4 %collective-permute-done.51 = bf16[2,64,1]{2,1,0:T(8,128)(2,1)S(1)} collective-permute-done((bf16[2,64,1]{2,1,0:T(8,128)(2,1)S(1)}, bf16[2,64,1]{2,1,0:T(8,128)(2,1)S(1)}, u32[]{:S(2)}, u32[]{:S(2)}) %collective-permute-start.51) | collective-permute-done | bytes 288 | tf_op jit(solution)/shard_map/ppermute | solution.py:26
  294.4 5.1 %collective-permute-start.52 = (bf16[2,1,258]{2,1,0:T(2,128)(2,1)S(1)}, bf16[2,1,258]{2,1,0:T(2,128)(2,1)S(1)}, u32[]{:S(2)}, u32[]{:S(2)}) collective-permute-start(bf16[2,1,258]{2,1,0:T(2,128)(2,1)S(1)} %get-tuple-element.248), channel_id=1, source_target_pairs={{0,1},{1,2},{2,3},{3,4},{4,5},{5,6},{6,7},{7,8},{8,9},{9,10},{10,1... | collective-permute-start | bytes 3104 | tf_op jit(solution)/shard_map/ppermute | solution.py:25
  311.5 5.6 %collective-permute-done.55 = bf16[3,64,1]{2,1,0:T(8,128)(2,1)S(1)} collective-permute-done((bf16[3,64,1]{2,1,0:T(8,128)(2,1)S(1)}, bf16[3,64,1]{2,1,0:T(8,128)(2,1)S(1)}, u32[]{:S(2)}, u32[]{:S(2)}) %collective-permute-start.55) | collective-permute-done | bytes 416 | tf_op jit(solution)/shard_map/ppermute | solution.py:26
  317.2 4.8 %collective-permute-start.56 = (bf16[3,1,258]{2,1,0:T(2,128)(2,1)S(1)}, bf16[3,1,258]{2,1,0:T(2,128)(2,1)S(1)}, u32[]{:S(2)}, u32[]{:S(2)}) collective-permute-start(bf16[3,1,258]{2,1,0:T(2,128)(2,1)S(1)} %get-tuple-element.232), channel_id=1, source_target_pairs={{0,1},{1,2},{2,3},{3,4},{4,5},{5,6},{6,7},{7,8},{8,9},{9,10},{10,1... | collective-permute-start | bytes 4652 | tf_op jit(solution)/shard_map/ppermute | solution.py:25
  333.9 5.4 %collective-permute-done.59 = bf16[2,64,1]{2,1,0:T(8,128)(2,1)S(1)} collective-permute-done((bf16[2,64,1]{2,1,0:T(8,128)(2,1)S(1)}, bf16[2,64,1]{2,1,0:T(8,128)(2,1)S(1)}, u32[]{:S(2)}, u32[]{:S(2)}) %collective-permute-start.59) | collective-permute-done | bytes 288 | tf_op jit(solution)/shard_map/ppermute | solution.py:26
  339.4 5.8 %collective-permute-start.60 = (bf16[2,1,258]{2,1,0:T(2,128)(2,1)S(1)}, bf16[2,1,258]{2,1,0:T(2,128)(2,1)S(1)}, u32[]{:S(2)}, u32[]{:S(2)}) collective-permute-start(bf16[2,1,258]{2,1,0:T(2,128)(2,1)S(1)} %get-tuple-element.246), channel_id=1, source_target_pairs={{0,1},{1,2},{2,3},{3,4},{4,5},{5,6},{6,7},{7,8},{8,9},{9,10},{10,1... | collective-permute-start | bytes 3104 | tf_op jit(solution)/shard_map/ppermute | solution.py:25
  357.9 5.6 %collective-permute-done.63 = bf16[3,64,1]{2,1,0:T(8,128)(2,1)S(1)} collective-permute-done((bf16[3,64,1]{2,1,0:T(8,128)(2,1)S(1)}, bf16[3,64,1]{2,1,0:T(8,128)(2,1)S(1)}, u32[]{:S(2)}, u32[]{:S(2)}) %collective-permute-start.63) | collective-permute-done | bytes 416 | tf_op jit(solution)/shard_map/ppermute | solution.py:26
  (240 shorter events, 193.2 us)
Async XLA Ops:
  0.7 62.0 %collective-permute-start.9 = (bf16[2,2,64,256]{3,2,1,0:T(8,128)(2,1)}, bf16[2,2,64,256]{3,2,1,0:T(8,128)(2,1)S(1)}, u32[]{:S(2)}, u32[]{:S(2)}) collective-permute-start(bf16[2,2,64,256]{3,2,1,0:T(8,128)(2,1)} %param.24), channel_id=1, source_target_pairs={{0,1},{1,2},{2,3},{3,4},{4,5},{5,6},{6,7},{7,8},{8,9},{9,10},{10,1... | collective-permute-start | bytes 393224 | tf_op jit(solution)/shard_map/ppermute | solution.py:25
  5.7 57.3 %collective-permute-start.8 = (bf16[2,2,64,256]{3,2,1,0:T(8,128)(2,1)}, bf16[2,2,64,256]{3,2,1,0:T(8,128)(2,1)S(1)}, u32[]{:S(2)}, u32[]{:S(2)}) collective-permute-start(bf16[2,2,64,256]{3,2,1,0:T(8,128)(2,1)} %param.24), channel_id=1, source_target_pairs={{1,0},{2,1},{3,2},{4,3},{5,4},{6,5},{7,6},{8,7},{9,8},{10,9},{11,1... | collective-permute-start | bytes 393224 | tf_op jit(solution)/shard_map/ppermute | solution.py:26
  8.6 13.5 %collective-permute-start = (bf16[2,64,1]{2,1,0:T(8,128)(2,1)S(1)}, bf16[2,64,1]{2,1,0:T(8,128)(2,1)S(1)}, u32[]{:S(2)}, u32[]{:S(2)}) collective-permute-start(bf16[2,64,1]{2,1,0:T(8,128)(2,1)S(1)} %get-tuple-element.294), channel_id=1, source_target_pairs={{0,24},{24,48},{48,72},{72,96},{96,120},{120,144},{144,168},{168,1... | collective-permute-start | bytes 776 | tf_op jit(solution)/shard_map/ppermute | solution.py:25
  14.4 7.7 %collective-permute-start.1 = (bf16[2,64,1]{2,1,0:T(8,128)(2,1)S(1)}, bf16[2,64,1]{2,1,0:T(8,128)(2,1)S(1)}, u32[]{:S(2)}, u32[]{:S(2)}) collective-permute-start(bf16[2,64,1]{2,1,0:T(8,128)(2,1)S(1)} %get-tuple-element.295), channel_id=1, source_target_pairs={{24,0},{48,24},{72,48},{96,72},{120,96},{144,120},{168,144},{192,1... | collective-permute-start | bytes 776 | tf_op jit(solution)/shard_map/ppermute | solution.py:26
  22.2 7.0 %collective-permute-start.2 = (bf16[2,1,258]{2,1,0:T(2,128)(2,1)S(1)}, bf16[2,1,258]{2,1,0:T(2,128)(2,1)S(1)}, u32[]{:S(2)}, u32[]{:S(2)}) collective-permute-start(bf16[2,1,258]{2,1,0:T(2,128)(2,1)S(1)} %get-tuple-element.262), channel_id=1, source_target_pairs={{0,1},{1,2},{2,3},{3,4},{4,5},{5,6},{6,7},{7,8},{8,9},{9,10},{10,1... | collective-permute-start | bytes 3104 | tf_op jit(solution)/shard_map/ppermute | solution.py:25
  35.6 8.9 %collective-permute-start.4 = (bf16[3,64,1]{2,1,0:T(8,128)(2,1)S(1)}, bf16[3,64,1]{2,1,0:T(8,128)(2,1)S(1)}, u32[]{:S(2)}, u32[]{:S(2)}) collective-permute-start(bf16[3,64,1]{2,1,0:T(8,128)(2,1)S(1)} %get-tuple-element.278), channel_id=1, source_target_pairs={{0,24},{24,48},{48,72},{72,96},{96,120},{120,144},{144,168},{168,1... | collective-permute-start | bytes 1160 | tf_op jit(solution)/shard_map/ppermute | solution.py:25
  42.5 7.5 %collective-permute-start.5 = (bf16[3,64,1]{2,1,0:T(8,128)(2,1)S(1)}, bf16[3,64,1]{2,1,0:T(8,128)(2,1)S(1)}, u32[]{:S(2)}, u32[]{:S(2)}) collective-permute-start(bf16[3,64,1]{2,1,0:T(8,128)(2,1)S(1)} %get-tuple-element.279), channel_id=1, source_target_pairs={{24,0},{48,24},{72,48},{96,72},{120,96},{144,120},{168,144},{192,1... | collective-permute-start | bytes 1160 | tf_op jit(solution)/shard_map/ppermute | solution.py:26
  50.2 11.6 %collective-permute-start.6 = (bf16[3,1,258]{2,1,0:T(2,128)(2,1)S(1)}, bf16[3,1,258]{2,1,0:T(2,128)(2,1)S(1)}, u32[]{:S(2)}, u32[]{:S(2)}) collective-permute-start(bf16[3,1,258]{2,1,0:T(2,128)(2,1)S(1)} %get-tuple-element.244), channel_id=1, source_target_pairs={{0,1},{1,2},{2,3},{3,4},{4,5},{5,6},{6,7},{7,8},{8,9},{9,10},{10,1... | collective-permute-start | bytes 4652 | tf_op jit(solution)/shard_map/ppermute | solution.py:25
  53.3 9.2 %collective-permute-start.7 = (bf16[3,1,258]{2,1,0:T(2,128)(2,1)S(1)}, bf16[3,1,258]{2,1,0:T(2,128)(2,1)S(1)}, u32[]{:S(2)}, u32[]{:S(2)}) collective-permute-start(bf16[3,1,258]{2,1,0:T(2,128)(2,1)S(1)} %get-tuple-element.245), channel_id=1, source_target_pairs={{1,0},{2,1},{3,2},{4,3},{5,4},{6,5},{7,6},{8,7},{9,8},{10,9},{11,1... | collective-permute-start | bytes 4652 | tf_op jit(solution)/shard_map/ppermute | solution.py:26
  66.2 7.3 %collective-permute-start.11 = (bf16[2,64,1]{2,1,0:T(8,128)(2,1)S(1)}, bf16[2,64,1]{2,1,0:T(8,128)(2,1)S(1)}, u32[]{:S(2)}, u32[]{:S(2)}) collective-permute-start(bf16[2,64,1]{2,1,0:T(8,128)(2,1)S(1)} %get-tuple-element.293), channel_id=1, source_target_pairs={{24,0},{48,24},{72,48},{96,72},{120,96},{144,120},{168,144},{192,1... | collective-permute-start | bytes 776 | tf_op jit(solution)/shard_map/ppermute | solution.py:26
  73.7 10.1 %collective-permute-start.12 = (bf16[2,1,258]{2,1,0:T(2,128)(2,1)S(1)}, bf16[2,1,258]{2,1,0:T(2,128)(2,1)S(1)}, u32[]{:S(2)}, u32[]{:S(2)}) collective-permute-start(bf16[2,1,258]{2,1,0:T(2,128)(2,1)S(1)} %get-tuple-element.260), channel_id=1, source_target_pairs={{0,1},{1,2},{2,3},{3,4},{4,5},{5,6},{6,7},{7,8},{8,9},{9,10},{10,1... | collective-permute-start | bytes 3104 | tf_op jit(solution)/shard_map/ppermute | solution.py:25
  87.6 7.5 %collective-permute-start.15 = (bf16[3,64,1]{2,1,0:T(8,128)(2,1)S(1)}, bf16[3,64,1]{2,1,0:T(8,128)(2,1)S(1)}, u32[]{:S(2)}, u32[]{:S(2)}) collective-permute-start(bf16[3,64,1]{2,1,0:T(8,128)(2,1)S(1)} %get-tuple-element.277), channel_id=1, source_target_pairs={{24,0},{48,24},{72,48},{96,72},{120,96},{144,120},{168,144},{192,1... | collective-permute-start | bytes 1160 | tf_op jit(solution)/shard_map/ppermute | solution.py:26
  95.2 9.6 %collective-permute-start.16 = (bf16[3,1,258]{2,1,0:T(2,128)(2,1)S(1)}, bf16[3,1,258]{2,1,0:T(2,128)(2,1)S(1)}, u32[]{:S(2)}, u32[]{:S(2)}) collective-permute-start(bf16[3,1,258]{2,1,0:T(2,128)(2,1)S(1)} %get-tuple-element.242), channel_id=1, source_target_pairs={{0,1},{1,2},{2,3},{3,4},{4,5},{5,6},{6,7},{7,8},{8,9},{9,10},{10,1... | collective-permute-start | bytes 4652 | tf_op jit(solution)/shard_map/ppermute | solution.py:25
  98.4 7.2 %collective-permute-start.17 = (bf16[3,1,258]{2,1,0:T(2,128)(2,1)S(1)}, bf16[3,1,258]{2,1,0:T(2,128)(2,1)S(1)}, u32[]{:S(2)}, u32[]{:S(2)}) collective-permute-start(bf16[3,1,258]{2,1,0:T(2,128)(2,1)S(1)} %get-tuple-element.243), channel_id=1, source_target_pairs={{1,0},{2,1},{3,2},{4,3},{5,4},{6,5},{7,6},{8,7},{9,8},{10,9},{11,1... | collective-permute-start | bytes 4652 | tf_op jit(solution)/shard_map/ppermute | solution.py:26
  109.1 7.3 %collective-permute-start.19 = (bf16[2,64,1]{2,1,0:T(8,128)(2,1)S(1)}, bf16[2,64,1]{2,1,0:T(8,128)(2,1)S(1)}, u32[]{:S(2)}, u32[]{:S(2)}) collective-permute-start(bf16[2,64,1]{2,1,0:T(8,128)(2,1)S(1)} %get-tuple-element.291), channel_id=1, source_target_pairs={{24,0},{48,24},{72,48},{96,72},{120,96},{144,120},{168,144},{192,1... | collective-permute-start | bytes 776 | tf_op jit(solution)/shard_map/ppermute | solution.py:26
  116.5 9.3 %collective-permute-start.20 = (bf16[2,1,258]{2,1,0:T(2,128)(2,1)S(1)}, bf16[2,1,258]{2,1,0:T(2,128)(2,1)S(1)}, u32[]{:S(2)}, u32[]{:S(2)}) collective-permute-start(bf16[2,1,258]{2,1,0:T(2,128)(2,1)S(1)} %get-tuple-element.258), channel_id=1, source_target_pairs={{0,1},{1,2},{2,3},{3,4},{4,5},{5,6},{6,7},{7,8},{8,9},{9,10},{10,1... | collective-permute-start | bytes 3104 | tf_op jit(solution)/shard_map/ppermute | solution.py:25
  132.3 7.5 %collective-permute-start.23 = (bf16[3,64,1]{2,1,0:T(8,128)(2,1)S(1)}, bf16[3,64,1]{2,1,0:T(8,128)(2,1)S(1)}, u32[]{:S(2)}, u32[]{:S(2)}) collective-permute-start(bf16[3,64,1]{2,1,0:T(8,128)(2,1)S(1)} %get-tuple-element.275), channel_id=1, source_target_pairs={{24,0},{48,24},{72,48},{96,72},{120,96},{144,120},{168,144},{192,1... | collective-permute-start | bytes 1160 | tf_op jit(solution)/shard_map/ppermute | solution.py:26
  139.9 7.7 %collective-permute-start.24 = (bf16[3,1,258]{2,1,0:T(2,128)(2,1)S(1)}, bf16[3,1,258]{2,1,0:T(2,128)(2,1)S(1)}, u32[]{:S(2)}, u32[]{:S(2)}) collective-permute-start(bf16[3,1,258]{2,1,0:T(2,128)(2,1)S(1)} %get-tuple-element.240), channel_id=1, source_target_pairs={{0,1},{1,2},{2,3},{3,4},{4,5},{5,6},{6,7},{7,8},{8,9},{9,10},{10,1... | collective-permute-start | bytes 4652 | tf_op jit(solution)/shard_map/ppermute | solution.py:25
  155.7 7.3 %collective-permute-start.27 = (bf16[2,64,1]{2,1,0:T(8,128)(2,1)S(1)}, bf16[2,64,1]{2,1,0:T(8,128)(2,1)S(1)}, u32[]{:S(2)}, u32[]{:S(2)}) collective-permute-start(bf16[2,64,1]{2,1,0:T(8,128)(2,1)S(1)} %get-tuple-element.289), channel_id=1, source_target_pairs={{24,0},{48,24},{72,48},{96,72},{120,96},{144,120},{168,144},{192,1... | collective-permute-start | bytes 776 | tf_op jit(solution)/shard_map/ppermute | solution.py:26
  163.1 7.7 %collective-permute-start.28 = (bf16[2,1,258]{2,1,0:T(2,128)(2,1)S(1)}, bf16[2,1,258]{2,1,0:T(2,128)(2,1)S(1)}, u32[]{:S(2)}, u32[]{:S(2)}) collective-permute-start(bf16[2,1,258]{2,1,0:T(2,128)(2,1)S(1)} %get-tuple-element.256), channel_id=1, source_target_pairs={{0,1},{1,2},{2,3},{3,4},{4,5},{5,6},{6,7},{7,8},{8,9},{9,10},{10,1... | collective-permute-start | bytes 3104 | tf_op jit(solution)/shard_map/ppermute | solution.py:25
  178.9 7.5 %collective-permute-start.31 = (bf16[3,64,1]{2,1,0:T(8,128)(2,1)S(1)}, bf16[3,64,1]{2,1,0:T(8,128)(2,1)S(1)}, u32[]{:S(2)}, u32[]{:S(2)}) collective-permute-start(bf16[3,64,1]{2,1,0:T(8,128)(2,1)S(1)} %get-tuple-element.273), channel_id=1, source_target_pairs={{24,0},{48,24},{72,48},{96,72},{120,96},{144,120},{168,144},{192,1... | collective-permute-start | bytes 1160 | tf_op jit(solution)/shard_map/ppermute | solution.py:26
  199.9 7.3 %collective-permute-start.35 = (bf16[2,64,1]{2,1,0:T(8,128)(2,1)S(1)}, bf16[2,64,1]{2,1,0:T(8,128)(2,1)S(1)}, u32[]{:S(2)}, u32[]{:S(2)}) collective-permute-start(bf16[2,64,1]{2,1,0:T(8,128)(2,1)S(1)} %get-tuple-element.287), channel_id=1, source_target_pairs={{24,0},{48,24},{72,48},{96,72},{120,96},{144,120},{168,144},{192,1... | collective-permute-start | bytes 776 | tf_op jit(solution)/shard_map/ppermute | solution.py:26
  221.8 7.5 %collective-permute-start.39 = (bf16[3,64,1]{2,1,0:T(8,128)(2,1)S(1)}, bf16[3,64,1]{2,1,0:T(8,128)(2,1)S(1)}, u32[]{:S(2)}, u32[]{:S(2)}) collective-permute-start(bf16[3,64,1]{2,1,0:T(8,128)(2,1)S(1)} %get-tuple-element.271), channel_id=1, source_target_pairs={{24,0},{48,24},{72,48},{96,72},{120,96},{144,120},{168,144},{192,1... | collective-permute-start | bytes 1160 | tf_op jit(solution)/shard_map/ppermute | solution.py:26
  242.7 7.3 %collective-permute-start.43 = (bf16[2,64,1]{2,1,0:T(8,128)(2,1)S(1)}, bf16[2,64,1]{2,1,0:T(8,128)(2,1)S(1)}, u32[]{:S(2)}, u32[]{:S(2)}) collective-permute-start(bf16[2,64,1]{2,1,0:T(8,128)(2,1)S(1)} %get-tuple-element.285), channel_id=1, source_target_pairs={{24,0},{48,24},{72,48},{96,72},{120,96},{144,120},{168,144},{192,1... | collective-permute-start | bytes 776 | tf_op jit(solution)/shard_map/ppermute | solution.py:26
  250.2 7.3 %collective-permute-start.44 = (bf16[2,1,258]{2,1,0:T(2,128)(2,1)S(1)}, bf16[2,1,258]{2,1,0:T(2,128)(2,1)S(1)}, u32[]{:S(2)}, u32[]{:S(2)}) collective-permute-start(bf16[2,1,258]{2,1,0:T(2,128)(2,1)S(1)} %get-tuple-element.250), channel_id=1, source_target_pairs={{0,1},{1,2},{2,3},{3,4},{4,5},{5,6},{6,7},{7,8},{8,9},{9,10},{10,1... | collective-permute-start | bytes 3104 | tf_op jit(solution)/shard_map/ppermute | solution.py:25
  265.6 7.5 %collective-permute-start.47 = (bf16[3,64,1]{2,1,0:T(8,128)(2,1)S(1)}, bf16[3,64,1]{2,1,0:T(8,128)(2,1)S(1)}, u32[]{:S(2)}, u32[]{:S(2)}) collective-permute-start(bf16[3,64,1]{2,1,0:T(8,128)(2,1)S(1)} %get-tuple-element.269), channel_id=1, source_target_pairs={{24,0},{48,24},{72,48},{96,72},{120,96},{144,120},{168,144},{192,1... | collective-permute-start | bytes 1160 | tf_op jit(solution)/shard_map/ppermute | solution.py:26
  286.9 7.3 %collective-permute-start.51 = (bf16[2,64,1]{2,1,0:T(8,128)(2,1)S(1)}, bf16[2,64,1]{2,1,0:T(8,128)(2,1)S(1)}, u32[]{:S(2)}, u32[]{:S(2)}) collective-permute-start(bf16[2,64,1]{2,1,0:T(8,128)(2,1)S(1)} %get-tuple-element.283), channel_id=1, source_target_pairs={{24,0},{48,24},{72,48},{96,72},{120,96},{144,120},{168,144},{192,1... | collective-permute-start | bytes 776 | tf_op jit(solution)/shard_map/ppermute | solution.py:26
  294.4 7.1 %collective-permute-start.52 = (bf16[2,1,258]{2,1,0:T(2,128)(2,1)S(1)}, bf16[2,1,258]{2,1,0:T(2,128)(2,1)S(1)}, u32[]{:S(2)}, u32[]{:S(2)}) collective-permute-start(bf16[2,1,258]{2,1,0:T(2,128)(2,1)S(1)} %get-tuple-element.248), channel_id=1, source_target_pairs={{0,1},{1,2},{2,3},{3,4},{4,5},{5,6},{6,7},{7,8},{8,9},{9,10},{10,1... | collective-permute-start | bytes 3104 | tf_op jit(solution)/shard_map/ppermute | solution.py:25
  309.6 7.5 %collective-permute-start.55 = (bf16[3,64,1]{2,1,0:T(8,128)(2,1)S(1)}, bf16[3,64,1]{2,1,0:T(8,128)(2,1)S(1)}, u32[]{:S(2)}, u32[]{:S(2)}) collective-permute-start(bf16[3,64,1]{2,1,0:T(8,128)(2,1)S(1)} %get-tuple-element.267), channel_id=1, source_target_pairs={{24,0},{48,24},{72,48},{96,72},{120,96},{144,120},{168,144},{192,1... | collective-permute-start | bytes 1160 | tf_op jit(solution)/shard_map/ppermute | solution.py:26
  332.0 7.3 %collective-permute-start.59 = (bf16[2,64,1]{2,1,0:T(8,128)(2,1)S(1)}, bf16[2,64,1]{2,1,0:T(8,128)(2,1)S(1)}, u32[]{:S(2)}, u32[]{:S(2)}) collective-permute-start(bf16[2,64,1]{2,1,0:T(8,128)(2,1)S(1)} %get-tuple-element.281), channel_id=1, source_target_pairs={{24,0},{48,24},{72,48},{96,72},{120,96},{144,120},{168,144},{192,1... | collective-permute-start | bytes 776 | tf_op jit(solution)/shard_map/ppermute | solution.py:26
  339.4 7.7 %collective-permute-start.60 = (bf16[2,1,258]{2,1,0:T(2,128)(2,1)S(1)}, bf16[2,1,258]{2,1,0:T(2,128)(2,1)S(1)}, u32[]{:S(2)}, u32[]{:S(2)}) collective-permute-start(bf16[2,1,258]{2,1,0:T(2,128)(2,1)S(1)} %get-tuple-element.246), channel_id=1, source_target_pairs={{0,1},{1,2},{2,3},{3,4},{4,5},{5,6},{6,7},{7,8},{8,9},{9,10},{10,1... | collective-permute-start | bytes 3104 | tf_op jit(solution)/shard_map/ppermute | solution.py:25
  355.9 7.5 %collective-permute-start.63 = (bf16[3,64,1]{2,1,0:T(8,128)(2,1)S(1)}, bf16[3,64,1]{2,1,0:T(8,128)(2,1)S(1)}, u32[]{:S(2)}, u32[]{:S(2)}) collective-permute-start(bf16[3,64,1]{2,1,0:T(8,128)(2,1)S(1)} %get-tuple-element.265), channel_id=1, source_target_pairs={{24,0},{48,24},{72,48},{96,72},{120,96},{144,120},{168,144},{192,1... | collective-permute-start | bytes 1160 | tf_op jit(solution)/shard_map/ppermute | solution.py:26
  (42 other events, 276.0 us)
where the time goes:
time: 377 us; the launch traced here: 375 us
  starting transfers between devices  214 us (57%)
  waiting for transfers between devices  140 us (37%)
  other arithmetic  11.9 us (3%)
  local copies, waits for them, and re-layouts  4.28 us (1%)
    ppermute x33, waiting for transfers between devices, padded(): after = lax.ppermute(leading, axis, down)  140 us
    ppermute x33, starting transfers between devices, padded(): before = lax.ppermute(last, axis, up)  128 us
    ppermute x33, starting transfers between devices, padded(): after = lax.ppermute(leading, axis, down)  86.3 us
  transfers between devices with their start and end apart: 66, of which 31 were waited for; matrix products, arithmetic and copies ran while one was open for 2% of the time, Pallas kernels for 0%

commit v1 on v0

v1 whole, which is shorter than its diff:
```python
import jax
import jax.numpy as jnp
from jax import lax
from jax.experimental import pallas as pl
from jax.experimental.pallas import tpu as pltpu
from jax.sharding import PartitionSpec as P

MESH = pl.DeviceIdType.MESH
F32 = jnp.float32
BF16 = jnp.bfloat16

ROWS = 64
LANES = 128
DEEP = 16
PAD = 8
BASE = PAD + DEEP
TALL = ROWS + 2 * BASE
SUB = 4
CATS = 6

U, V, X, Y, S, B0, E0, B1, E1, GX0, GY0, GX1, GY1 = range(13)
STATE = ((U,), (V,), (X,), (Y,), (S,), (B0,), (E0,), (B1, E1))
FORCE0 = ((GX0,), (GY0,))
FORCE1 = ((GX1, GY1),)


def lane_ids(rows):
    return lax.broadcasted_iota(jnp.int32, (rows, LANES), 1)


def turn(value, shift):
    shift = shift % LANES
    return pltpu.roll(value, shift, 1) if shift else value


def pack_sides(ext, rim, edge, blocks):
    top, low = BASE + ROWS - DEEP, BASE
    for k, block in enumerate(blocks):
        for c in range(2):
            if len(block) == 1:
                rim[0, k, c] = ext[block[0], c, top : top + DEEP, :].astype(BF16)
                rim[1, k, c] = ext[block[0], c, low : low + DEEP, :].astype(BF16)
            else:
                one, two = block
                half = DEEP // 2
                rim[0, k, c] = jnp.concatenate(
                    [ext[one, c, top + half : top + DEEP, :], ext[two, c, top + half : top + DEEP, :]], axis=0
                ).astype(BF16)
                rim[1, k, c] = jnp.concatenate(
                    [ext[one, c, low : low + half, :], ext[two, c, low : low + half, :]], axis=0
                ).astype(BF16)
    lanes = lane_ids(DEEP)
    for piece in range(ROWS // DEEP):
        rows = slice(BASE + piece * DEEP, BASE + (piece + 1) * DEEP)
        east = jnp.zeros((DEEP, LANES), F32)
        west = jnp.zeros((DEEP, LANES), F32)
        for k, block in enumerate(blocks):
            width = DEEP // len(block)
            for part, field in enumerate(block):
                start = DEEP * k + width * part
                here = (lanes >= start) & (lanes < start + width)
                east = jnp.where(here, turn(ext[field, 1, rows, :], start - (LANES - width)), east)
                west = jnp.where(here, turn(ext[field, 0, rows, :], start), west)
        edge[0, piece * DEEP : (piece + 1) * DEEP, :] = east.astype(BF16)
        edge[1, piece * DEEP : (piece + 1) * DEEP, :] = west.astype(BF16)


def unpack_sides(ext, rim, edge, blocks, north_in, south_in):
    for k, block in enumerate(blocks):
        for c in range(2):
            from_north = rim[0, k, c].astype(F32) * north_in
            from_south = rim[1, k, c].astype(F32) * south_in
            top, low = BASE + ROWS, BASE - DEEP
            if len(block) == 1:
                ext[block[0], c, top : top + DEEP, :] = from_north
                ext[block[0], c, low : low + DEEP, :] = from_south
            else:
                half = DEEP // 2
                for part, field in enumerate(block):
                    ext[field, c, top : top + half, :] = from_north[part * half : (part + 1) * half]
                    ext[field, c, low + half : low + DEEP, :] = from_south[part * half : (part + 1) * half]
    left = lane_ids(DEEP) < LANES // 2
    pieces = ROWS // DEEP + 2
    for piece in range(pieces):
        rows = slice(piece * DEEP, (piece + 1) * DEEP)
        east = edge[0, rows, :].astype(F32)
        west = edge[1, rows, :].astype(F32)
        if piece == 0:
            east, west = east * south_in, west * south_in
        if piece == pieces - 1:
            east, west = east * north_in, west * north_in
        for k, block in enumerate(blocks):
            width = DEEP // len(block)
            for part, field in enumerate(block):
                start = DEEP * k + width * part
                ext[field, 2, PAD + piece * DEEP : PAD + (piece + 1) * DEEP, :] = jnp.where(
                    left, turn(east, -start), turn(west, LANES - width - start)
                )


def side_copies(rim_out, edge_out, rim_in, edge_in, send, recv, lat, lon, lats, lons):
    north, south = lax.rem(lat + 1, lats), lax.rem(lat + lats - 1, lats)
    east, west = lax.rem(lon + 1, lons), lax.rem(lon + lons - 1, lons)
    tail, end = pl.ds(ROWS - DEEP, DEEP), pl.ds(ROWS + DEEP, DEEP)
    head, body = pl.ds(0, DEEP), pl.ds(DEEP, ROWS)
    plan = (
        (rim_out.at[0], rim_in.at[1], north, lon),
        (rim_out.at[1], rim_in.at[0], south, lon),
        (edge_out.at[0], edge_in.at[1, body], lat, east),
        (edge_out.at[1], edge_in.at[0, body], lat, west),
        (edge_out.at[0, tail], edge_in.at[1, head], north, east),
        (edge_out.at[1, tail], edge_in.at[0, head], north, west),
        (edge_out.at[0, head], edge_in.at[1, end], south, east),
        (edge_out.at[1, head], edge_in.at[0, end], south, west),
    )
    return [
        pltpu.make_async_remote_copy(
            src_ref=source,
            dst_ref=target,
            send_sem=send.at[i],
            recv_sem=recv.at[i],
            device_id={"lat": to_lat, "lon": to_lon},
            device_id_type=MESH,
        )
        for i, (source, target, to_lat, to_lon) in enumerate(plan)
    ]


def spread(tiles, first, last):
    ahead = [turn(t, -1) for t in tiles]
    behind = [turn(t, 1) for t in tiles]
    return [
        jnp.where(last, ahead[(c + 1) % 3], ahead[c]) - jnp.where(first, behind[(c + 2) % 3], behind[c])
        for c in range(3)
    ]


def stress_rows(ext, row, bulk, mass, first, last):
    def at(field, shift):
        return [ext[field, c, pl.ds(row + shift, 8), :] for c in range(3)]

    du = spread(at(U, 0), first, last)
    dv = spread(at(V, 0), first, last)
    un, us, vn, vs = at(U, 1), at(U, -1), at(V, 1), at(V, -1)
    for c in range(3):
        rows = pl.ds(row, 8)
        up = vn[c] - vs[c]
        shear = (un[c] - us[c]) + dv[c]
        div = du[c] + up
        ten = du[c] - up
        rate = lax.rsqrt(div * div + 0.25 * (ten * ten + shear * shear) + 1.0)
        b = ext[bulk, c, rows, :]
        keep = jnp.where(ext[mass, c, rows, :] > 0.0, 2.0 / 3.0, 0.0)
        br = b * rate
        quarter = 0.25 * br
        press = br * div - b
        pull = quarter * ten
        ext[X, c, rows, :] = (keep * ext[X, c, rows, :] + press) + pull
        ext[Y, c, rows, :] = (keep * ext[Y, c, rows, :] + press) - pull
        ext[S, c, rows, :] = keep * ext[S, c, rows, :] + quarter * shear


def velocity_rows(ext, row, mass, gx, gy, first, last):
    def at(field, shift):
        return [ext[field, c, pl.ds(row + shift, 8), :] for c in range(3)]

    dx = spread(at(X, 0), first, last)
    ds = spread(at(S, 0), first, last)
    yn, ys, sn, ss = at(Y, 1), at(Y, -1), at(S, 1), at(S, -1)
    for c in range(3):
        rows = pl.ds(row, 8)
        e = ext[mass, c, rows, :]
        keep = jnp.where(e > 0.0, 1.0 - e, 0.0)
        fx = dx[c] + (sn[c] - ss[c])
        fy = ds[c] + (yn[c] - ys[c])
        ext[U, c, rows, :] = keep * ext[U, c, rows, :] + (ext[gx, c, rows, :] + e * fx)
        ext[V, c, rows, :] = keep * ext[V, c, rows, :] + (ext[gy, c, rows, :] + e * fy)


def tiles_within(reach):
    above = (reach + 7) // 8
    return BASE // 8 - above, BASE // 8 + ROWS // 8 + above


def sweep(low, high, body):
    def step(i, carry):
        body(pl.multiple_of(i * 8, 8))
        return carry

    lax.fori_loop(low, high, step, 0)


def kernel(
    vel_hbm,
    str_hbm,
    thk_hbm,
    con_hbm,
    land_hbm,
    cov_hbm,
    oce_hbm,
    win_hbm,
    reg_hbm,
    off_hbm,
    vel_out,
    str_out,
    thk_out,
    vel,
    stress,
    thk,
    con,
    land,
    cov,
    oce,
    win,
    reg,
    off,
    ext,
    rim_a_out,
    edge_a_out,
    rim_a_in,
    edge_a_in,
    rim_b_out,
    edge_b_out,
    rim_b_in,
    edge_b_in,
    rim_c_out,
    edge_c_out,
    rim_c_in,
    edge_c_in,
    load_sem,
    send_a,
    recv_a,
    send_b,
    recv_b,
    send_c,
    recv_c,
    send_o,
    recv_o,
):
    lat, lon = lax.axis_index("lat"), lax.axis_index("lon")
    lats, lons = lax.axis_size("lat"), lax.axis_size("lon")
    north, south = lax.rem(lat + 1, lats), lax.rem(lat + lats - 1, lats)
    east, west = lax.rem(lon + 1, lons), lax.rem(lon + lons - 1, lons)

    barrier = pltpu.get_barrier_semaphore()
    around = ((north, lon), (south, lon), (lat, east), (lat, west), (north, east), (north, west), (south, east), (south, west))
    for to_lat, to_lon in around:
        pl.semaphore_signal(barrier, inc=1, device_id={"lat": to_lat, "lon": to_lon}, device_id_type=MESH)

    loads = [
        pltpu.make_async_copy(source, target, load_sem.at[i])
        for i, (source, target) in enumerate(
            (
                (vel_hbm, vel),
                (str_hbm, stress),
                (thk_hbm, thk),
                (con_hbm, con),
                (land_hbm, land),
                (cov_hbm, cov),
                (win_hbm, win),
                (reg_hbm, reg),
                (off_hbm, off),
                (oce_hbm, oce.at[:, :, pl.ds(0, ROWS), :]),
            )
        )
    ]
    for load in loads:
        load.start()
    ocean = []
    for w in range(2):
        for d, (target, slot) in enumerate(((north, 2), (south, 1))):
            ocean.append(
                pltpu.make_async_remote_copy(
                    src_ref=oce_hbm.at[w],
                    dst_ref=oce.at[w, :, pl.ds(slot * ROWS, ROWS), :],
                    send_sem=send_o.at[2 * w + d],
                    recv_sem=recv_o.at[2 * w + d],
                    device_id={"lat": target, "lon": lon},
                    device_id_type=MESH,
                )
            )
    pl.semaphore_wait(barrier, len(around))
    ocean[0].start()
    ocean[1].start()

    for load in loads[:6]:
        load.wait()

    lanes_one = lane_ids(1)[:, : cov.shape[1]]
    flags = [
        jnp.sum(jnp.where(lanes_one == 2 * lon + c, cov[...], 0), axis=1, keepdims=True) > 0 for c in range(2)
    ]

    def prepare(i, carry):
        row = pl.multiple_of(i * 8, 8)
        rows = pl.ds(row, 8)
        inner = pl.ds(pl.multiple_of(BASE + row, 8), 8)
        for c in range(2):
            cells = slice(c * LANES, (c + 1) * LANES)
            ext[U, c, inner, :] = vel[0, rows, cells]
            ext[V, c, inner, :] = vel[1, rows, cells]
            one, two = stress[0, rows, cells], stress[1, rows, cells]
            ext[X, c, inner, :] = 0.25 * (one + two)
            ext[Y, c, inner, :] = 0.25 * (one - two)
            ext[S, c, inner, :] = 0.5 * stress[2, rows, cells]
            open_mask = land[rows, cells].astype(F32)
            share = [con[k, rows, cells] for k in range(CATS)]
            thick = [thk[k, rows, cells] for k in range(CATS)]
            area = sum(share[1:], share[0])
            weight = jnp.exp(-2.0 * (1.0 - area)) * open_mask * (1.0 / 12.0)
            volume = sum((share[k] * thick[k] for k in range(1, CATS)), share[0] * thick[0])
            grow = jnp.broadcast_to(flags[c], (8, LANES))
            for bulk, mass in ((B0, E0), (B1, E1)):
                mean = volume / area
                thick = [jnp.where(grow, t + 0.3 / (0.5 + t) + 0.3 * (mean - t), t) for t in thick]
                volume = sum((share[k] * thick[k] for k in range(1, CATS)), share[0] * thick[0])
                ext[bulk, c, inner, :] = volume * weight
                ext[mass, c, inner, :] = 0.5 * open_mask / (volume + 1.0)
            for k in range(CATS):
                thk_out[k, rows, cells] = thick[k]
        return carry

    lax.fori_loop(0, ROWS // 8, prepare, 0)

    pack_sides(ext, rim_a_out, edge_a_out, STATE)
    copies_a = side_copies(rim_a_out, edge_a_out, rim_a_in, edge_a_in, send_a, recv_a, lat, lon, lats, lons)
    for copy in copies_a:
        copy.start()
    ocean[2].start()
    ocean[3].start()

    for load in loads[6:]:
        load.wait()
    line = lax.broadcasted_iota(jnp.int32, (ROWS, ROWS), 0)
    mark = lax.broadcasted_iota(jnp.int32, (ROWS, ROWS), 1)
    upward = jnp.sum(jnp.where(line == mark, jnp.broadcast_to(off[...], (ROWS, ROWS)), 0), axis=1, keepdims=True) > 0
    upward = jnp.broadcast_to(upward, (ROWS, LANES))
    weights = reg[...].astype(F32)
    high = jnp.where((lane_ids(ROWS) < ROWS) | upward, weights, 0.0).astype(BF16)
    deep = jnp.where(upward, 0.0, turn(weights, ROWS)).astype(BF16)[:, :ROWS]

    def force(w, mass, fields):
        for part, field in enumerate(fields):
            current = jnp.dot(high, oce[w, part, : 2 * ROWS, :], preferred_element_type=F32)
            current = current + jnp.dot(deep, oce[w, part, 2 * ROWS :, :], preferred_element_type=F32)
            total = current + win[w, part].astype(F32)
            for c in range(2):
                inner = slice(BASE, BASE + ROWS)
                ext[field, c, inner, :] = ext[mass, c, inner, :] * total[:, c * LANES : (c + 1) * LANES]

    north_in = jnp.where(lat == lats - 1, 0.0, 1.0).astype(F32)
    south_in = jnp.where(lat == 0, 0.0, 1.0).astype(F32)

    ocean[0].wait_recv()
    ocean[1].wait_recv()
    force(0, E0, (GX0, GY0))
    pack_sides(ext, rim_b_out, edge_b_out, FORCE0)
    copies_b = side_copies(rim_b_out, edge_b_out, rim_b_in, edge_b_in, send_b, recv_b, lat, lon, lats, lons)
    for copy in copies_b:
        copy.start()

    for copy in copies_a:
        copy.wait_recv()
    unpack_sides(ext, rim_a_in, edge_a_in, STATE, north_in, south_in)

    ocean[2].wait_recv()
    ocean[3].wait_recv()
    force(1, E1, (GX1, GY1))
    pack_sides(ext, rim_c_out, edge_c_out, FORCE1)
    copies_c = side_copies(rim_c_out, edge_c_out, rim_c_in, edge_c_in, send_c, recv_c, lat, lon, lats, lons)
    for copy in copies_c:
        copy.start()

    lanes = lane_ids(8)
    first, last = lanes == 0, lanes == LANES - 1
    settings = ((B0, E0, GX0, GY0, copies_b, rim_b_in, edge_b_in, FORCE0), (B1, E1, GX1, GY1, copies_c, rim_c_in, edge_c_in, FORCE1))
    reach = DEEP
    for bulk, mass, gx, gy, copies, rim_in, edge_in, blocks in settings:
        for step in range(SUB):
            low, high_row = tiles_within(reach - 1)
            sweep(low, high_row, lambda row: stress_rows(ext, row, bulk, mass, first, last))
            if step == 0:
                for copy in copies:
                    copy.wait_recv()
                unpack_sides(ext, rim_in, edge_in, blocks, north_in, south_in)
            low, high_row = tiles_within(reach - 2)
            sweep(low, high_row, lambda row: velocity_rows(ext, row, mass, gx, gy, first, last))
            reach -= 2

    for c in range(2):
        cells = slice(c * LANES, (c + 1) * LANES)
        inner = slice(BASE, BASE + ROWS)
        vel_out[0, :, cells] = ext[U, c, inner, :]
        vel_out[1, :, cells] = ext[V, c, inner, :]
        one, two = ext[X, c, inner, :], ext[Y, c, inner, :]
        str_out[0, :, cells] = 2.0 * (one + two)
        str_out[1, :, cells] = 2.0 * (one - two)
        str_out[2, :, cells] = 2.0 * ext[S, c, inner, :]

    for copy in ocean + copies_a + copies_b + copies_c:
        copy.wait_send()


def local(velocity, stress, thickness, concentration, land_mask, covered, ocean_current, wind_stress, regrid_weights, tile_offset):
    offsets = tile_offset.reshape(1, -1)
    arrays = (velocity, stress, thickness, concentration, land_mask, covered, ocean_current, wind_stress, regrid_weights, offsets)
    width = velocity.shape[-1]
    ocean_rows = (2, 2, 3 * ROWS, width)

    def rim(blocks):
        return pltpu.VMEM((2, len(blocks), 2, DEEP, LANES), BF16)

    edge_out = pltpu.VMEM((2, ROWS, LANES), BF16)
    edge_in = pltpu.VMEM((2, ROWS + 2 * DEEP, LANES), BF16)
    staged = [
        pltpu.VMEM(ocean_rows if i == 6 else a.shape, a.dtype) for i, a in enumerate(arrays)
    ]
    sides = [item for blocks in (STATE, FORCE0, FORCE1) for item in (rim(blocks), edge_out, rim(blocks), edge_in)]
    dma = pltpu.SemaphoreType.DMA
    return pl.pallas_call(
        kernel,
        out_shape=(
            jax.ShapeDtypeStruct(velocity.shape, F32),
            jax.ShapeDtypeStruct(stress.shape, F32),
            jax.ShapeDtypeStruct(thickness.shape, F32),
        ),
        in_specs=[pl.BlockSpec(memory_space=pl.ANY)] * len(arrays),
        out_specs=[pl.BlockSpec(memory_space=pltpu.VMEM)] * 3,
        scratch_shapes=staged
        + [pltpu.VMEM((13, 3, TALL, LANES), F32)]
        + sides
        + [dma((10,)), dma((8,)), dma((8,)), dma((8,)), dma((8,)), dma((8,)), dma((8,)), dma((4,)), dma((4,))],
        compiler_params=pltpu.CompilerParams(collective_id=0, has_side_effects=True),
    )(*arrays)


def solution(mesh):
    return jax.shard_map(
        local,
        mesh=mesh,
        in_specs=(
            P(None, "lat", "lon"),
            P(None, "lat", "lon"),
            P(None, "lat", "lon"),
            P(None, "lat", "lon"),
            P("lat", "lon"),
            P("lat", None),
            P(None, None, "lat", "lon"),
            P(None, None, "lat", "lon"),
            P("lat", None),
            P("lat"),
        ),
        out_specs=(P(None, "lat", "lon"), P(None, "lat", "lon"), P(None, "lat", "lon")),
        check_vma=False,
    )
```

time: 377 us -> 53.1 us (0.14)
  the two profiles are of different devices: /device:TPU:31 before, /device:TPU:1 now
where the time goes in v1:
time: 53.1 us; the launch traced here: 52.9 us
  Pallas kernels  48.3 us (91%)
  local copies, waits for them, and re-layouts  3.98 us (7%)
  between operations  0.65 us (1%)
    pallas_call x1, Pallas kernels, local(): pl.pallas_call(kernel, out_shape=(jax.ShapeDtypeStruct(velocity.shape, F3...  48.3 us
    unnamed x5, local copies, waits for them, and re-layouts  3.98 us

profile of v1, /device:TPU:1, one launch (start us, length us, event | category | flops | bytes accessed | tf_op | source)
XLA Modules:
  0.0 52.9 jit_solution(13261472205910223036)
XLA Ops:
  0.6 48.3 %shard_map.121 = (f32[2,64,256]{2,1,0:T(8,128)}, f32[3,64,256]{2,1,0:T(8,128)}, f32[6,64,256]{2,1,0:T(8,128)}) custom-call(f32[2,64,256]{2,1,0:T(8,128)} %vel_hbm.1, f32[3,64,256]{2,1,0:T(8,128)} %str_hbm.1, f32[6,64,256]{2,1,0:T(8,128)} %thk_hbm.1, f32[6,64,256]{2,1,0:T(8,128)} %con_hbm.1, s32[64,256]{1,0:T(8,128)} %land_hbm.1, s32[1,64]{1,0:T(1,128)} %cov_hbm.1, ...), custom_call_target="tpu_custom_call" | custom-call | tf_op jit(solution)/shard_map/pallas_call | solution.py:420
  49.0 0.0 copy-start
  49.0 1.6 %copy.16 = f32[2,64,256]{2,1,0:T(8,128)} copy(f32[2,64,256]{2,1,0:T(8,128)} %get-tuple-element.6) | data formatting | bytes 262144
  50.6 1.6 %copy.17 = f32[3,64,256]{2,1,0:T(8,128)} copy(f32[3,64,256]{2,1,0:T(8,128)} %get-tuple-element.7) | data formatting | bytes 393216
  52.2 0.0 copy-done
  52.2 0.7 %copy.18 = f32[6,64,256]{2,1,0:T(8,128)} copy(f32[6,64,256]{2,1,0:T(8,128)S(1)} %copy-done) | data formatting | bytes 786432
Async XLA Ops:
  49.0 3.2 %copy-start = (f32[6,64,256]{2,1,0:T(8,128)S(1)}, f32[6,64,256]{2,1,0:T(8,128)}, u32[]{:S(2)}) copy-start(f32[6,64,256]{2,1,0:T(8,128)} %get-tuple-element.8) | copy-start | bytes 1179652

commit v2 on v1

v2 whole, which is shorter than its diff:
```python
import jax
import jax.numpy as jnp
from jax import lax
from jax.experimental import pallas as pl
from jax.experimental.pallas import tpu as pltpu
from jax.sharding import PartitionSpec as P

MESH = pl.DeviceIdType.MESH
F32 = jnp.float32
BF16 = jnp.bfloat16

ROWS = 64
LANES = 128
DEEP = 16
PAD = 8
BASE = PAD + DEEP
TALL = ROWS + 2 * BASE
SUB = 4
CATS = 6

U, V, X, Y, S, B0, E0, B1, E1, GX0, GY0, GX1, GY1 = range(13)
STATE = ((U,), (V,), (X,), (Y,), (S,), (B0,), (E0,), (B1, E1))
WIDE = ROWS + 2 * DEEP
NEAR = (-2, -1, 0, 1, 2)
GROUP = 2


def lane_ids(rows):
    return lax.broadcasted_iota(jnp.int32, (rows, LANES), 1)


def turn(value, shift):
    shift = shift % LANES
    return pltpu.roll(value, shift, 1) if shift else value


def pack_sides(ext, rim, edge):
    top, low = BASE + ROWS - DEEP, BASE
    half = DEEP // 2
    for k, block in enumerate(STATE):
        for c in range(2):
            if len(block) == 1:
                rim[0, k, c] = ext[block[0]][c, top : top + DEEP, :].astype(BF16)
                rim[1, k, c] = ext[block[0]][c, low : low + DEEP, :].astype(BF16)
            else:
                one, two = ext[block[0]], ext[block[1]]
                rim[0, k, c] = jnp.concatenate([one[c, top + half : top + DEEP, :], two[c, top + half : top + DEEP, :]], axis=0).astype(BF16)
                rim[1, k, c] = jnp.concatenate([one[c, low : low + half, :], two[c, low : low + half, :]], axis=0).astype(BF16)
    lanes = lane_ids(DEEP)
    for piece in range(ROWS // DEEP):
        rows = slice(BASE + piece * DEEP, BASE + (piece + 1) * DEEP)
        east = jnp.zeros((DEEP, LANES), F32)
        west = jnp.zeros((DEEP, LANES), F32)
        for k, block in enumerate(STATE):
            width = DEEP // len(block)
            for part, field in enumerate(block):
                start = DEEP * k + width * part
                here = (lanes >= start) & (lanes < start + width)
                east = jnp.where(here, turn(ext[field][1, rows, :], start - (LANES - width)), east)
                west = jnp.where(here, turn(ext[field][0, rows, :], start), west)
        edge[0, piece * DEEP : (piece + 1) * DEEP, :] = east.astype(BF16)
        edge[1, piece * DEEP : (piece + 1) * DEEP, :] = west.astype(BF16)


def unpack_sides(ext, rim, edge, north_in, south_in):
    half = DEEP // 2
    top, low = BASE + ROWS, BASE - DEEP
    for k, block in enumerate(STATE):
        for c in range(2):
            from_north = rim[0, k, c].astype(F32) * north_in
            from_south = rim[1, k, c].astype(F32) * south_in
            if len(block) == 1:
                ext[block[0]][c, top : top + DEEP, :] = from_north
                ext[block[0]][c, low : low + DEEP, :] = from_south
            else:
                for part, field in enumerate(block):
                    ext[field][c, top : top + half, :] = from_north[part * half : (part + 1) * half]
                    ext[field][c, low + half : low + DEEP, :] = from_south[part * half : (part + 1) * half]
    left = lane_ids(DEEP) < LANES // 2
    pieces = WIDE // DEEP
    for piece in range(pieces):
        rows = slice(piece * DEEP, (piece + 1) * DEEP)
        east = edge[0, rows, :].astype(F32)
        west = edge[1, rows, :].astype(F32)
        if piece == 0:
            east, west = east * south_in, west * south_in
        if piece == pieces - 1:
            east, west = east * north_in, west * north_in
        for k, block in enumerate(STATE):
            width = DEEP // len(block)
            for part, field in enumerate(block):
                start = DEEP * k + width * part
                ext[field][2, PAD + piece * DEEP : PAD + (piece + 1) * DEEP, :] = jnp.where(
                    left, turn(east, -start), turn(west, LANES - width - start)
                )


def pack_ocean(ocean, wind, side):
    lanes = lane_ids(ROWS)
    east = jnp.zeros((ROWS, LANES), F32)
    west = jnp.zeros((ROWS, LANES), F32)
    for k in range(8):
        w, part = (k % 4) // 2, k % 2
        if k < 4:
            field = ocean[w, part, 2 * ROWS : 3 * ROWS, :]
        else:
            field = wind[w, part, DEEP : DEEP + ROWS, :]
        start = DEEP * k
        here = (lanes >= start) & (lanes < start + DEEP)
        east = jnp.where(here, turn(field[:, LANES:].astype(F32), start + DEEP), east)
        west = jnp.where(here, turn(field[:, :LANES].astype(F32), start), west)
    side[0] = east.astype(BF16)
    side[1] = west.astype(BF16)


def spread(tiles, first, last):
    ahead = [turn(t, -1) for t in tiles]
    behind = [turn(t, 1) for t in tiles]
    return [
        jnp.where(last, ahead[(c + 1) % 3], ahead[c]) - jnp.where(first, behind[(c + 2) % 3], behind[c])
        for c in range(3)
    ]


def stress_rows(ext, rows_list, bulk, mass, first, last):
    results = []
    for row in rows_list:

        def at(field, shift):
            return [ext[field][c, pl.ds(row + shift, 8), :] for c in range(3)]

        du = spread(at(U, 0), first, last)
        dv = spread(at(V, 0), first, last)
        un, us, vn, vs = at(U, 1), at(U, -1), at(V, 1), at(V, -1)
        bs, es, xs, ys, ss = at(bulk, 0), at(mass, 0), at(X, 0), at(Y, 0), at(S, 0)
        for c in range(3):
            up = vn[c] - vs[c]
            shear = (un[c] - us[c]) + dv[c]
            div = du[c] + up
            ten = du[c] - up
            rate = lax.rsqrt(div * div + 0.25 * (ten * ten + shear * shear) + 1.0)
            keep = jnp.where(es[c] > 0.0, 2.0 / 3.0, 0.0)
            br = bs[c] * rate
            quarter = 0.25 * br
            press = br * div - bs[c]
            pull = quarter * ten
            common = keep * xs[c] + press
            other = keep * ys[c] + press
            results.append((row, c, common + pull, other - pull, keep * ss[c] + quarter * shear))
    for row, c, x, y, s in results:
        rows = pl.ds(row, 8)
        ext[X][c, rows, :] = x
        ext[Y][c, rows, :] = y
        ext[S][c, rows, :] = s


def velocity_rows(ext, rows_list, mass, gx, gy, first, last):
    results = []
    for row in rows_list:

        def at(field, shift):
            return [ext[field][c, pl.ds(row + shift, 8), :] for c in range(3)]

        dx = spread(at(X, 0), first, last)
        ds = spread(at(S, 0), first, last)
        yn, ys, sn, ss = at(Y, 1), at(Y, -1), at(S, 1), at(S, -1)
        es, us, vs, gxs, gys = at(mass, 0), at(U, 0), at(V, 0), at(gx, 0), at(gy, 0)
        for c in range(3):
            e = es[c]
            keep = jnp.where(e > 0.0, 1.0 - e, 0.0)
            fx = dx[c] + (sn[c] - ss[c])
            fy = ds[c] + (yn[c] - ys[c])
            results.append((row, c, keep * us[c] + (gxs[c] + e * fx), keep * vs[c] + (gys[c] + e * fy)))
    for row, c, u, v in results:
        rows = pl.ds(row, 8)
        ext[U][c, rows, :] = u
        ext[V][c, rows, :] = v


def tiles_within(reach):
    above = (reach + 7) // 8
    return BASE // 8 - above, BASE // 8 + ROWS // 8 + above


def sweep(low, high, body):
    def step(i, carry):
        start = pl.multiple_of((low + i * GROUP) * 8, 8)
        body([start + 8 * j for j in range(GROUP)])
        return carry

    lax.fori_loop(0, (high - low) // GROUP, step, 0)


def kernel(
    vel_hbm,
    str_hbm,
    thk_hbm,
    con_hbm,
    land_hbm,
    cov_hbm,
    oce_hbm,
    win_hbm,
    reg_hbm,
    off_hbm,
    vel_out,
    str_out,
    thk_out,
    vel,
    stress,
    thk,
    con,
    land,
    cov,
    oce,
    win,
    reg,
    off,
    u_ref,
    v_ref,
    x_ref,
    y_ref,
    s_ref,
    b0_ref,
    e0_ref,
    b1_ref,
    e1_ref,
    gx0_ref,
    gy0_ref,
    gx1_ref,
    gy1_ref,
    rim_out,
    edge_out,
    rim_in,
    edge_in,
    side_out,
    side_in,
    mix_out,
    mix_in,
    mix,
    load_sem,
    send_a,
    recv_a,
    send_o,
    recv_o,
    send_s,
    recv_s,
    send_m,
    recv_m,
):
    ext = (u_ref, v_ref, x_ref, y_ref, s_ref, b0_ref, e0_ref, b1_ref, e1_ref, gx0_ref, gy0_ref, gx1_ref, gy1_ref)
    lat, lon = lax.axis_index("lat"), lax.axis_index("lon")
    lats, lons = lax.axis_size("lat"), lax.axis_size("lon")

    def place(up, right):
        return lax.rem(lat + lats + up, lats), lax.rem(lon + lons + right, lons)

    def send_to(up, right, source, target, send, recv):
        to_lat, to_lon = place(up, right)
        return pltpu.make_async_remote_copy(
            src_ref=source,
            dst_ref=target,
            send_sem=send,
            recv_sem=recv,
            device_id={"lat": to_lat, "lon": to_lon},
            device_id_type=MESH,
        )

    barrier = pltpu.get_barrier_semaphore()
    around = [(up, right) for up in NEAR for right in (-1, 0, 1) if up or right]
    for up, right in around:
        to_lat, to_lon = place(up, right)
        pl.semaphore_signal(barrier, inc=1, device_id={"lat": to_lat, "lon": to_lon}, device_id_type=MESH)

    own = pl.ds(2 * ROWS, ROWS)
    loads = [
        pltpu.make_async_copy(source, target, load_sem.at[i])
        for i, (source, target) in enumerate(
            (
                (oce_hbm, oce.at[:, :, own, :]),
                (win_hbm, win.at[:, :, pl.ds(DEEP, ROWS), :]),
                (reg_hbm, reg),
                (off_hbm, off),
                (thk_hbm, thk),
                (con_hbm, con),
                (land_hbm, land),
                (cov_hbm, cov),
                (vel_hbm, vel),
                (str_hbm, stress),
            )
        )
    ]
    for load in loads:
        load.start()

    tail, head = pl.ds(ROWS - DEEP, DEEP), pl.ds(0, DEEP)
    ocean = [
        [
            send_to(
                up,
                0,
                oce_hbm.at[w],
                oce.at[w, :, pl.ds((2 - up) * ROWS, ROWS), :],
                send_o.at[4 * w + i],
                recv_o.at[4 * w + i],
            )
            for i, up in enumerate((1, -1, 2, -2))
        ]
        for w in range(2)
    ]
    winds = [
        send_to(1, 0, win_hbm.at[:, :, tail, :], win.at[:, :, pl.ds(0, DEEP), :], send_m.at[0], recv_m.at[0]),
        send_to(-1, 0, win_hbm.at[:, :, head, :], win.at[:, :, pl.ds(DEEP + ROWS, DEEP), :], send_m.at[1], recv_m.at[1]),
    ]
    mixes = [
        send_to(1, 0, mix_out.at[tail], mix_in.at[0], send_m.at[2], recv_m.at[2]),
        send_to(-1, 0, mix_out.at[head], mix_in.at[1], send_m.at[3], recv_m.at[3]),
    ]
    sides = [
        send_to(
            up,
            right,
            side_out.at[0 if right > 0 else 1],
            side_in.at[0 if right > 0 else 1, pl.ds((2 - up) * ROWS, ROWS), :],
            send_s.at[i],
            recv_s.at[i],
        )
        for i, (up, right) in enumerate((up, right) for up in NEAR for right in (-1, 1))
    ]
    end, body = pl.ds(ROWS + DEEP, DEEP), pl.ds(DEEP, ROWS)
    halo = [
        send_to(up, right, source, target, send_a.at[i], recv_a.at[i])
        for i, (up, right, source, target) in enumerate(
            (
                (1, 0, rim_out.at[0], rim_in.at[1]),
                (-1, 0, rim_out.at[1], rim_in.at[0]),
                (0, 1, edge_out.at[0], edge_in.at[1, body]),
                (0, -1, edge_out.at[1], edge_in.at[0, body]),
                (1, 1, edge_out.at[0, tail], edge_in.at[1, head]),
                (1, -1, edge_out.at[1, tail], edge_in.at[0, head]),
                (-1, 1, edge_out.at[0, head], edge_in.at[1, end]),
                (-1, -1, edge_out.at[1, head], edge_in.at[0, end]),
            )
        )
    ]

    pl.semaphore_wait(barrier, len(around))
    for copy in ocean[0] + winds:
        copy.start()

    for load in loads[:4]:
        load.wait()
    pack_ocean(oce, win, side_out)
    for copy in sides:
        copy.start()

    line = lax.broadcasted_iota(jnp.int32, (ROWS, ROWS), 0)
    mark = lax.broadcasted_iota(jnp.int32, (ROWS, ROWS), 1)
    upward = jnp.sum(jnp.where(line == mark, jnp.broadcast_to(off[...], (ROWS, ROWS)), 0), axis=1, keepdims=True) > 0
    upward = jnp.broadcast_to(upward, (ROWS, LANES))
    weights = turn(reg[...].astype(F32), ROWS)
    left = lane_ids(ROWS) < ROWS
    lower = jnp.where(left & upward, 0.0, weights)
    upper = jnp.where(left & upward, weights, 0.0)
    mix_out[:, :LANES] = lower.astype(BF16)
    mix_out[:, LANES:] = upper.astype(BF16)
    for copy in mixes:
        copy.start()
    lower, upper = turn(lower, ROWS), turn(upper, ROWS)
    inner = slice(DEEP, DEEP + ROWS)
    mix[inner, :LANES] = jnp.where(left, 0.0, lower).astype(BF16)
    mix[inner, LANES : 2 * LANES] = jnp.where(left, lower, upper).astype(BF16)
    mix[inner, 2 * LANES :] = jnp.zeros((ROWS, LANES), BF16)

    for load in loads[4:]:
        load.wait()

    lanes_one = lane_ids(1)[:, : cov.shape[1]]
    flags = [
        jnp.sum(jnp.where(lanes_one == 2 * lon + c, cov[...], 0), axis=1, keepdims=True) > 0 for c in range(2)
    ]

    def prepare(i, carry):
        row = pl.multiple_of(i * 8, 8)
        rows = pl.ds(row, 8)
        inside = pl.ds(pl.multiple_of(BASE + row, 8), 8)
        for c in range(2):
            cells = slice(c * LANES, (c + 1) * LANES)
            ext[U][c, inside, :] = vel[0, rows, cells]
            ext[V][c, inside, :] = vel[1, rows, cells]
            one, two = stress[0, rows, cells], stress[1, rows, cells]
            ext[X][c, inside, :] = 0.25 * (one + two)
            ext[Y][c, inside, :] = 0.25 * (one - two)
            ext[S][c, inside, :] = 0.5 * stress[2, rows, cells]
            open_mask = land[rows, cells].astype(F32)
            share = [con[k, rows, cells] for k in range(CATS)]
            thick = [thk[k, rows, cells] for k in range(CATS)]
            area = sum(share[1:], share[0])
            weight = jnp.exp(-2.0 * (1.0 - area)) * open_mask * (1.0 / 12.0)
            volume = sum((share[k] * thick[k] for k in range(1, CATS)), share[0] * thick[0])
            grow = jnp.broadcast_to(flags[c], (8, LANES))
            for bulk, mass in ((B0, E0), (B1, E1)):
                mean = volume / area
                thick = [jnp.where(grow, t + 0.3 / (0.5 + t) + 0.3 * (mean - t), t) for t in thick]
                volume = sum((share[k] * thick[k] for k in range(1, CATS)), share[0] * thick[0])
                ext[bulk][c, inside, :] = volume * weight
                ext[mass][c, inside, :] = 0.5 * open_mask / (volume + 1.0)
            for k in range(CATS):
                thk_out[k, rows, cells] = thick[k]
        return carry

    lax.fori_loop(0, ROWS // 8, prepare, 0)

    pack_sides(ext, rim_out, edge_out)
    for copy in halo + ocean[1]:
        copy.start()

    north_in = jnp.where(lat == lats - 1, 0.0, 1.0).astype(F32)
    south_in = jnp.where(lat == 0, 0.0, 1.0).astype(F32)
    lanes = lane_ids(8)
    first, last = lanes == 0, lanes == LANES - 1
    band = slice(PAD, PAD + WIDE)

    def force(w, mass, fields):
        for part, field in enumerate(fields):
            current = jnp.dot(mix[:, : 5 * ROWS], oce[w, part], preferred_element_type=F32)
            total = current + win[w, part].astype(F32)
            for c in range(2):
                ext[field][c, band, :] = ext[mass][c, band, :] * total[:, c * LANES : (c + 1) * LANES]

    for copy in halo:
        copy.wait_recv()
    unpack_sides(ext, rim_in, edge_in, north_in, south_in)

    reach = DEEP
    for bulk, mass, gx, gy in ((B0, E0, GX0, GY0), (B1, E1, GX1, GY1)):
        for step in range(SUB):
            low, high = tiles_within(reach - 1)
            sweep(low, high, lambda rows: stress_rows(ext, rows, bulk, mass, first, last))
            if step == 0 and bulk == B0:
                for copy in mixes:
                    copy.wait_recv()
                mix[:DEEP, : 2 * LANES] = mix_in[0]
                mix[:DEEP, 2 * LANES :] = jnp.zeros((DEEP, LANES), BF16)
                mix[DEEP + ROWS :, :LANES] = jnp.zeros((DEEP, LANES), BF16)
                mix[DEEP + ROWS :, LANES:] = mix_in[1]
                for copy in sides:
                    copy.wait_recv()
                near = slice(2 * ROWS - DEEP, 3 * ROWS + DEEP)
                flows = [
                    jnp.dot(mix[:, : 5 * ROWS], side_in[d], preferred_element_type=F32)
                    + turn(side_in[d, near, :].astype(F32), ROWS)
                    for d in range(2)
                ]
                is_east = lane_ids(WIDE) < LANES // 2
                for k, (field, weight) in enumerate(((GX0, E0), (GY0, E0), (GX1, E1), (GY1, E1))):
                    total = jnp.where(is_east, turn(flows[1], -DEEP * k), turn(flows[0], LANES - DEEP - DEEP * k))
                    ext[field][2, band, :] = ext[weight][2, band, :] * total
                for copy in winds + ocean[0]:
                    copy.wait_recv()
                force(0, E0, (GX0, GY0))
            if step == 0 and bulk == B1:
                for copy in ocean[1]:
                    copy.wait_recv()
                force(1, E1, (GX1, GY1))
            low, high = tiles_within(reach - 2)
            sweep(low, high, lambda rows: velocity_rows(ext, rows, mass, gx, gy, first, last))
            reach -= 2

    inner = slice(BASE, BASE + ROWS)
    for c in range(2):
        cells = slice(c * LANES, (c + 1) * LANES)
        one, two = ext[X][c, inner, :], ext[Y][c, inner, :]
        str_out[0, :, cells] = 2.0 * (one + two)
        str_out[1, :, cells] = 2.0 * (one - two)
        str_out[2, :, cells] = 2.0 * ext[S][c, inner, :]
        vel_out[0, :, cells] = ext[U][c, inner, :]
        vel_out[1, :, cells] = ext[V][c, inner, :]

    for copy in ocean[0] + ocean[1] + winds + mixes + sides + halo:
        copy.wait_send()


def local(velocity, stress, thickness, concentration, land_mask, covered, ocean_current, wind_stress, regrid_weights, tile_offset):
    offsets = tile_offset.reshape(1, -1)
    arrays = (velocity, stress, thickness, concentration, land_mask, covered, ocean_current, wind_stress, regrid_weights, offsets)
    width = velocity.shape[-1]
    held = {6: (2, 2, 5 * ROWS, width), 7: (2, 2, WIDE, width)}
    staged = [pltpu.VMEM(held.get(i, a.shape), a.dtype) for i, a in enumerate(arrays)]
    field = pltpu.VMEM((3, TALL, LANES), F32)
    rim = pltpu.VMEM((2, len(STATE), 2, DEEP, LANES), BF16)
    dma = pltpu.SemaphoreType.DMA
    return pl.pallas_call(
        kernel,
        out_shape=[pltpu.VMEM(a.shape, F32) for a in (velocity, stress, thickness)],
        in_specs=[pl.BlockSpec(memory_space=pl.ANY)] * len(arrays),
        out_specs=[pl.BlockSpec(memory_space=pltpu.VMEM)] * 3,
        scratch_shapes=staged
        + [field] * 13
        + [
            rim,
            pltpu.VMEM((2, ROWS, LANES), BF16),
            rim,
            pltpu.VMEM((2, WIDE, LANES), BF16),
            pltpu.VMEM((2, ROWS, LANES), BF16),
            pltpu.VMEM((2, 5 * ROWS, LANES), BF16),
            pltpu.VMEM((ROWS, 2 * LANES), BF16),
            pltpu.VMEM((2, DEEP, 2 * LANES), BF16),
            pltpu.VMEM((WIDE, 3 * LANES), BF16),
        ]
        + [dma((n,)) for n in (10, 8, 8, 8, 8, 10, 10, 4, 4)],
        compiler_params=pltpu.CompilerParams(collective_id=0, has_side_effects=True),
    )(*arrays)


def solution(mesh):
    return jax.shard_map(
        local,
        mesh=mesh,
        in_specs=(
            P(None, "lat", "lon"),
            P(None, "lat", "lon"),
            P(None, "lat", "lon"),
            P(None, "lat", "lon"),
            P("lat", "lon"),
            P("lat", None),
            P(None, None, "lat", "lon"),
            P(None, None, "lat", "lon"),
            P("lat", None),
            P("lat"),
        ),
        out_specs=(P(None, "lat", "lon"), P(None, "lat", "lon"), P(None, "lat", "lon")),
        check_vma=False,
    )
```

time: 53.1 us -> 44.5 us (0.84)
  Pallas kernels: 48.3 us -> 41.7 us
  local copies, waits for them, and re-layouts: 3.98 us -> 2.08 us
    pallas_call x1, Pallas kernels: 48.3 us -> 41.7 us  [local(): pl.pallas_call(kernel, out_shape=[pltpu.VMEM(a.shape, F32) for a in (velo...]
    unnamed x5 -> x3, local copies, waits for them, and re-layouts: 3.98 us -> 2.08 us
where the time goes in v2:
time: 44.5 us; the launch traced here: 44.4 us
  Pallas kernels  41.7 us (94%)
  local copies, waits for them, and re-layouts  2.08 us (5%)
  between operations  0.64 us (1%)
    pallas_call x1, Pallas kernels, local(): pl.pallas_call(kernel, out_shape=[pltpu.VMEM(a.shape, F32) for a in (velo...  41.7 us
    unnamed x3, local copies, waits for them, and re-layouts  2.08 us

profile of v2, /device:TPU:1, one launch (start us, length us, event | category | flops | bytes accessed | tf_op | source)
XLA Modules:
  0.0 44.4 jit_solution(493141815015761400)
XLA Ops:
  0.6 41.7 %shard_map.121 = (f32[2,64,256]{2,1,0:T(8,128)S(1)}, f32[3,64,256]{2,1,0:T(8,128)S(1)}, f32[6,64,256]{2,1,0:T(8,128)S(1)}) custom-call(f32[2,64,256]{2,1,0:T(8,128)} %vel_hbm.1, f32[3,64,256]{2,1,0:T(8,128)} %str_hbm.1, f32[6,64,256]{2,1,0:T(8,128)} %thk_hbm.1, f32[6,64,256]{2,1,0:T(8,128)} %con_hbm.1, s32[64,256]{1,0:T(8,128)} %land_hbm.1, ...), custom_call_target="tpu_custom_call" | custom-call | tf_op jit(solution)/shard_map/pallas_call | solution.py:492
  42.3 0.7 %copy.16 = f32[2,64,256]{2,1,0:T(8,128)} copy(f32[2,64,256]{2,1,0:T(8,128)S(1)} %get-tuple-element.3) | data formatting | bytes 262144
  43.0 0.7 %copy.17 = f32[3,64,256]{2,1,0:T(8,128)} copy(f32[3,64,256]{2,1,0:T(8,128)S(1)} %get-tuple-element.4) | data formatting | bytes 393216
  43.6 0.7 %copy.18 = f32[6,64,256]{2,1,0:T(8,128)} copy(f32[6,64,256]{2,1,0:T(8,128)S(1)} %get-tuple-element.5) | data formatting | bytes 786432

commit v3 on v2

--- a/solution.py
+++ b/solution.py
@@ -62,13 +62,13 @@
         edge[1, piece * DEEP : (piece + 1) * DEEP, :] = west.astype(BF16)
 
 
-def unpack_sides(ext, rim, edge, north_in, south_in):
+def unpack_sides(ext, rim, edge):
     half = DEEP // 2
     top, low = BASE + ROWS, BASE - DEEP
     for k, block in enumerate(STATE):
         for c in range(2):
-            from_north = rim[0, k, c].astype(F32) * north_in
-            from_south = rim[1, k, c].astype(F32) * south_in
+            from_north = rim[0, k, c].astype(F32)
+            from_south = rim[1, k, c].astype(F32)
             if len(block) == 1:
                 ext[block[0]][c, top : top + DEEP, :] = from_north
                 ext[block[0]][c, low : low + DEEP, :] = from_south
@@ -82,10 +82,6 @@
         rows = slice(piece * DEEP, (piece + 1) * DEEP)
         east = edge[0, rows, :].astype(F32)
         west = edge[1, rows, :].astype(F32)
-        if piece == 0:
-            east, west = east * south_in, west * south_in
-        if piece == pieces - 1:
-            east, west = east * north_in, west * north_in
         for k, block in enumerate(STATE):
             width = DEEP // len(block)
             for part, field in enumerate(block):
@@ -183,12 +179,8 @@
 
 
 def sweep(low, high, body):
-    def step(i, carry):
-        start = pl.multiple_of((low + i * GROUP) * 8, 8)
-        body([start + 8 * j for j in range(GROUP)])
-        return carry
-
-    lax.fori_loop(0, (high - low) // GROUP, step, 0)
+    for start in range(low, high, GROUP):
+        body([8 * tile for tile in range(start, min(start + GROUP, high))])
 
 
 def kernel(
@@ -256,7 +248,7 @@
 
     def send_to(up, right, source, target, send, recv):
         to_lat, to_lon = place(up, right)
-        return pltpu.make_async_remote_copy(
+        return up, pltpu.make_async_remote_copy(
             src_ref=source,
             dst_ref=target,
             send_sem=send,
@@ -265,11 +257,40 @@
             device_id_type=MESH,
         )
 
+    def begin(copies):
+        for up, copy in copies:
+            only_if(up, copy.start)
+
+    def arrive(copies):
+        for up, copy in copies:
+            only_if(-up, copy.wait_recv)
+
+    def leave(copies):
+        for up, copy in copies:
+            only_if(up, copy.wait_send)
+
+    def exists(up):
+        return lat + up < lats if up > 0 else lat + up >= 0
+
+    def only_if(up, act):
+        if up:
+            pl.when(exists(up))(act)
+        else:
+            act()
+
     barrier = pltpu.get_barrier_semaphore()
-    around = [(up, right) for up in NEAR for right in (-1, 0, 1) if up or right]
-    for up, right in around:
-        to_lat, to_lon = place(up, right)
-        pl.semaphore_signal(barrier, inc=1, device_id={"lat": to_lat, "lon": to_lon}, device_id_type=MESH)
+    greeted = jnp.int32(2)
+    for up in NEAR:
+
+        def greet(up=up):
+            for right in (-1, 0, 1):
+                if up or right:
+                    to_lat, to_lon = place(up, right)
+                    pl.semaphore_signal(barrier, inc=1, device_id={"lat": to_lat, "lon": to_lon}, device_id_type=MESH)
+
+        only_if(up, greet)
+        if up:
+            greeted = greeted + jnp.where(exists(up), 3, 0)
 
     own = pl.ds(2 * ROWS, ROWS)
     loads = [
@@ -343,15 +364,27 @@
         )
     ]
 
-    pl.semaphore_wait(barrier, len(around))
-    for copy in ocean[0] + winds:
-        copy.start()
+    pl.semaphore_wait(barrier, greeted)
+    begin(ocean[0] + winds)
+
+    def blank(up, parts):
+        @pl.when(jnp.logical_not(exists(up)))
+        def _():
+            for part in parts:
+                part[...] = jnp.zeros(part.shape, part.dtype)
+
+    for up, outer, inner_block in ((-1, pl.ds(0, DEEP), 1), (1, pl.ds(DEEP + ROWS, DEEP), 3)):
+        beside = pl.ds(inner_block * ROWS, ROWS)
+        side = 1 if up < 0 else 0
+        blank(up, (rim_in.at[side], edge_in.at[:, outer, :], win.at[:, :, outer, :], mix_in.at[1 - side], oce.at[:, :, beside, :], side_in.at[:, beside, :]))
+    for up, block in ((-2, 0), (2, 4)):
+        beyond = pl.ds(block * ROWS, ROWS)
+        blank(up, (oce.at[:, :, beyond, :], side_in.at[:, beyond, :]))
 
     for load in loads[:4]:
         load.wait()
     pack_ocean(oce, win, side_out)
-    for copy in sides:
-        copy.start()
+    begin(sides)
 
     line = lax.broadcasted_iota(jnp.int32, (ROWS, ROWS), 0)
     mark = lax.broadcasted_iota(jnp.int32, (ROWS, ROWS), 1)
@@ -363,8 +396,7 @@
     upper = jnp.where(left & upward, weights, 0.0)
     mix_out[:, :LANES] = lower.astype(BF16)
     mix_out[:, LANES:] = upper.astype(BF16)
-    for copy in mixes:
-        copy.start()
+    begin(mixes)
     lower, upper = turn(lower, ROWS), turn(upper, ROWS)
     inner = slice(DEEP, DEEP + ROWS)
     mix[inner, :LANES] = jnp.where(left, 0.0, lower).astype(BF16)
@@ -411,11 +443,8 @@
     lax.fori_loop(0, ROWS // 8, prepare, 0)
 
     pack_sides(ext, rim_out, edge_out)
-    for copy in halo + ocean[1]:
-        copy.start()
-
-    north_in = jnp.where(lat == lats - 1, 0.0, 1.0).astype(F32)
-    south_in = jnp.where(lat == 0, 0.0, 1.0).astype(F32)
+    begin(halo + ocean[1])
+
     lanes = lane_ids(8)
     first, last = lanes == 0, lanes == LANES - 1
     band = slice(PAD, PAD + WIDE)
@@ -427,9 +456,8 @@
             for c in range(2):
                 ext[field][c, band, :] = ext[mass][c, band, :] * total[:, c * LANES : (c + 1) * LANES]
 
-    for copy in halo:
-        copy.wait_recv()
-    unpack_sides(ext, rim_in, edge_in, north_in, south_in)
+    arrive(halo)
+    unpack_sides(ext, rim_in, edge_in)
 
     reach = DEEP
     for bulk, mass, gx, gy in ((B0, E0, GX0, GY0), (B1, E1, GX1, GY1)):
@@ -437,14 +465,12 @@
             low, high = tiles_within(reach - 1)
             sweep(low, high, lambda rows: stress_rows(ext, rows, bulk, mass, first, last))
             if step == 0 and bulk == B0:
-                for copy in mixes:
-                    copy.wait_recv()
+                arrive(mixes)
                 mix[:DEEP, : 2 * LANES] = mix_in[0]
                 mix[:DEEP, 2 * LANES :] = jnp.zeros((DEEP, LANES), BF16)
                 mix[DEEP + ROWS :, :LANES] = jnp.zeros((DEEP, LANES), BF16)
                 mix[DEEP + ROWS :, LANES:] = mix_in[1]
-                for copy in sides:
-                    copy.wait_recv()
+                arrive(sides)
                 near = slice(2 * ROWS - DEEP, 3 * ROWS + DEEP)
                 flows = [
                     jnp.dot(mix[:, : 5 * ROWS], side_in[d], preferred_element_type=F32)
@@ -455,12 +481,10 @@
                 for k, (field, weight) in enumerate(((GX0, E0), (GY0, E0), (GX1, E1), (GY1, E1))):
                     total = jnp.where(is_east, turn(flows[1], -DEEP * k), turn(flows[0], LANES - DEEP - DEEP * k))
                     ext[field][2, band, :] = ext[weight][2, band, :] * total
-                for copy in winds + ocean[0]:
-                    copy.wait_recv()
+                arrive(winds + ocean[0])
                 force(0, E0, (GX0, GY0))
             if step == 0 and bulk == B1:
-                for copy in ocean[1]:
-                    copy.wait_recv()
+                arrive(ocean[1])
                 force(1, E1, (GX1, GY1))
             low, high = tiles_within(reach - 2)
             sweep(low, high, lambda rows: velocity_rows(ext, rows, mass, gx, gy, first, last))
@@ -476,8 +500,7 @@
         vel_out[0, :, cells] = ext[U][c, inner, :]
         vel_out[1, :, cells] = ext[V][c, inner, :]
 
-    for copy in ocean[0] + ocean[1] + winds + mixes + sides + halo:
-        copy.wait_send()
+    leave(ocean[0] + ocean[1] + winds + mixes + sides + halo)
 
 
 def local(velocity, stress, thickness, concentration, land_mask, covered, ocean_current, wind_stress, regrid_weights, tile_offset):

time: 44.5 us -> 29.3 us (0.66)
  the two profiles are of different devices: /device:TPU:1 before, /device:TPU:5 now
where the time goes in v3:
time: 29.3 us; the launch traced here: 29.2 us
  Pallas kernels  26.4 us (90%)
  local copies, waits for them, and re-layouts  2.08 us (7%)
  between operations  0.64 us (2%)
    pallas_call x1, Pallas kernels, local(): pl.pallas_call(kernel, out_shape=[pltpu.VMEM(a.shape, F32) for a in (velo...  26.4 us
    unnamed x3, local copies, waits for them, and re-layouts  2.08 us

profile of v3, /device:TPU:5, one launch (start us, length us, event | category | flops | bytes accessed | tf_op | source)
XLA Modules:
  0.0 29.2 jit_solution(12393873875310128680)
XLA Ops:
  0.6 26.4 %shard_map.121 = (f32[2,64,256]{2,1,0:T(8,128)S(1)}, f32[3,64,256]{2,1,0:T(8,128)S(1)}, f32[6,64,256]{2,1,0:T(8,128)S(1)}) custom-call(f32[2,64,256]{2,1,0:T(8,128)} %vel_hbm.1, f32[3,64,256]{2,1,0:T(8,128)} %str_hbm.1, f32[6,64,256]{2,1,0:T(8,128)} %thk_hbm.1, f32[6,64,256]{2,1,0:T(8,128)} %con_hbm.1, s32[64,256]{1,0:T(8,128)} %land_hbm.1, ...), custom_call_target="tpu_custom_call" | custom-call | tf_op jit(solution)/shard_map/pallas_call | solution.py:515
  27.1 0.7 %copy.16 = f32[2,64,256]{2,1,0:T(8,128)} copy(f32[2,64,256]{2,1,0:T(8,128)S(1)} %get-tuple-element.3) | data formatting | bytes 262144
  27.7 0.7 %copy.17 = f32[3,64,256]{2,1,0:T(8,128)} copy(f32[3,64,256]{2,1,0:T(8,128)S(1)} %get-tuple-element.4) | data formatting | bytes 393216
  28.4 0.7 %copy.18 = f32[6,64,256]{2,1,0:T(8,128)} copy(f32[6,64,256]{2,1,0:T(8,128)S(1)} %get-tuple-element.5) | data formatting | bytes 786432

commit v4 on v3

--- a/solution.py
+++ b/solution.py
@@ -324,10 +324,23 @@
                 send_o.at[4 * w + i],
                 recv_o.at[4 * w + i],
             )
-            for i, up in enumerate((1, -1, 2, -2))
+            for i, up in enumerate((2, -2))
         ]
         for w in range(2)
     ]
+    stride = 1 - 2 * lax.rem(lat, 2)
+    given = pl.ds(pl.multiple_of((2 - stride) * ROWS, ROWS), ROWS)
+    taken = pl.ds(pl.multiple_of((2 + stride) * ROWS, ROWS), ROWS)
+    pairs = [
+        send_to(stride, 0, oce_hbm.at[w], oce.at[w, :, given, :], send_o.at[4 * w + 2], recv_o.at[4 * w + 2])[1]
+        for w in range(2)
+    ]
+    relays = [
+        send_to(2 * stride, 0, oce.at[w, :, taken, :], oce.at[w, :, given, :], send_o.at[4 * w + 3], recv_o.at[4 * w + 3])[1]
+        for w in range(2)
+    ]
+    passes_on = (lat + 2 * stride >= 0) & (lat + 2 * stride < lats)
+    is_passed = (lat - 2 * stride >= 0) & (lat - 2 * stride < lats)
     winds = [
         send_to(1, 0, win_hbm.at[:, :, tail, :], win.at[:, :, pl.ds(0, DEEP), :], send_m.at[0], recv_m.at[0]),
         send_to(-1, 0, win_hbm.at[:, :, head, :], win.at[:, :, pl.ds(DEEP + ROWS, DEEP), :], send_m.at[1], recv_m.at[1]),
@@ -365,7 +378,10 @@
     ]
 
     pl.semaphore_wait(barrier, greeted)
-    begin(ocean[0] + winds)
+    pairs[0].start()
+    begin(ocean[0])
+    pairs[1].start()
+    begin(ocean[1] + winds)
 
     def blank(up, parts):
         @pl.when(jnp.logical_not(exists(up)))
@@ -443,7 +459,10 @@
     lax.fori_loop(0, ROWS // 8, prepare, 0)
 
     pack_sides(ext, rim_out, edge_out)
-    begin(halo + ocean[1])
+    begin(halo)
+    for pair, relay in zip(pairs, relays):
+        pair.wait_recv()
+        pl.when(passes_on)(relay.start)
 
     lanes = lane_ids(8)
     first, last = lanes == 0, lanes == LANES - 1
@@ -482,9 +501,11 @@
                     total = jnp.where(is_east, turn(flows[1], -DEEP * k), turn(flows[0], LANES - DEEP - DEEP * k))
                     ext[field][2, band, :] = ext[weight][2, band, :] * total
                 arrive(winds + ocean[0])
+                pl.when(is_passed)(relays[0].wait_recv)
                 force(0, E0, (GX0, GY0))
             if step == 0 and bulk == B1:
                 arrive(ocean[1])
+                pl.when(is_passed)(relays[1].wait_recv)
                 force(1, E1, (GX1, GY1))
             low, high = tiles_within(reach - 2)
             sweep(low, high, lambda rows: velocity_rows(ext, rows, mass, gx, gy, first, last))
@@ -501,6 +522,20 @@
         vel_out[1, :, cells] = ext[V][c, inner, :]
 
     leave(ocean[0] + ocean[1] + winds + mixes + sides + halo)
+    for pair, relay in zip(pairs, relays):
+        pair.wait_send()
+        pl.when(passes_on)(relay.wait_send)
+
+
+def deliver(vel, stress, thick, vel_out, str_out, thk_out, sems):
+    copies = [
+        pltpu.make_async_copy(source, target, sems.at[i])
+        for i, (source, target) in enumerate(((vel, vel_out), (stress, str_out), (thick, thk_out)))
+    ]
+    for copy in copies:
+        copy.start()
+    for copy in copies:
+        copy.wait()
 
 
 def local(velocity, stress, thickness, concentration, land_mask, covered, ocean_current, wind_stress, regrid_weights, tile_offset):
@@ -512,7 +547,7 @@
     field = pltpu.VMEM((3, TALL, LANES), F32)
     rim = pltpu.VMEM((2, len(STATE), 2, DEEP, LANES), BF16)
     dma = pltpu.SemaphoreType.DMA
-    return pl.pallas_call(
+    results = pl.pallas_call(
         kernel,
         out_shape=[pltpu.VMEM(a.shape, F32) for a in (velocity, stress, thickness)],
         in_specs=[pl.BlockSpec(memory_space=pl.ANY)] * len(arrays),
@@ -534,6 +569,14 @@
         compiler_params=pltpu.CompilerParams(collective_id=0, has_side_effects=True),
     )(*arrays)
 
+    return pl.pallas_call(
+        deliver,
+        out_shape=[jax.ShapeDtypeStruct(a.shape, F32) for a in (velocity, stress, thickness)],
+        in_specs=[pl.BlockSpec(memory_space=pltpu.VMEM)] * 3,
+        out_specs=[pl.BlockSpec(memory_space=pl.ANY)] * 3,
+        scratch_shapes=[dma((3,))],
+    )(*[pltpu.with_memory_space_constraint(r, pltpu.VMEM) for r in results])
+
 
 def solution(mesh):
     return jax.shard_map(

time: 29.3 us -> 26.9 us (0.918)
  the two profiles are of different devices: /device:TPU:5 before, /device:TPU:1 now
where the time goes in v4:
time: 26.9 us; the launch traced here: 26.8 us
  Pallas kernels  26.1 us (97%)
  between operations  0.64 us (2%)
    pallas_call x1, Pallas kernels, local(): pl.pallas_call(kernel, out_shape=[pltpu.VMEM(a.shape, F32) for a in (velo...  25.2 us
    pallas_call x1, Pallas kernels, local(): pl.pallas_call(deliver, out_shape=[jax.ShapeDtypeStruct(a.shape, F32) for...  0.88 us

profile of v4, /device:TPU:1, one launch (start us, length us, event | category | flops | bytes accessed | tf_op | source)
XLA Modules:
  0.0 26.8 jit_solution(15225503316748519687)
XLA Ops:
  0.6 25.2 %shard_map.121 = (f32[2,64,256]{2,1,0:T(8,128)S(1)}, f32[3,64,256]{2,1,0:T(8,128)S(1)}, f32[6,64,256]{2,1,0:T(8,128)S(1)}) custom-call(f32[2,64,256]{2,1,0:T(8,128)} %vel_hbm.1, f32[3,64,256]{2,1,0:T(8,128)} %str_hbm.1, f32[6,64,256]{2,1,0:T(8,128)} %thk_hbm.1, f32[6,64,256]{2,1,0:T(8,128)} %con_hbm.1, s32[64,256]{1,0:T(8,128)} %land_hbm.1, ...), custom_call_target="tpu_custom_call" | custom-call | tf_op jit(solution)/shard_map/pallas_call | solution.py:550
  25.9 0.9 %shard_map.122 = (f32[2,64,256]{2,1,0:T(8,128)}, f32[3,64,256]{2,1,0:T(8,128)}, f32[6,64,256]{2,1,0:T(8,128)}) custom-call(f32[2,64,256]{2,1,0:T(8,128)S(1)} %get-tuple-element.6.vel, f32[3,64,256]{2,1,0:T(8,128)S(1)} %get-tuple-element.7.stress, f32[6,64,256]{2,1,0:T(8,128)S(1)} %get-tuple-element.8.thick), custom_call_target="tpu_custom_call" | custom-call | tf_op jit(solution)/shard_map/pallas_call | solution.py:572

commit v5 on v4

--- a/solution.py
+++ b/solution.py
@@ -400,7 +400,6 @@
     for load in loads[:4]:
         load.wait()
     pack_ocean(oce, win, side_out)
-    begin(sides)
 
     line = lax.broadcasted_iota(jnp.int32, (ROWS, ROWS), 0)
     mark = lax.broadcasted_iota(jnp.int32, (ROWS, ROWS), 1)
@@ -412,7 +411,6 @@
     upper = jnp.where(left & upward, weights, 0.0)
     mix_out[:, :LANES] = lower.astype(BF16)
     mix_out[:, LANES:] = upper.astype(BF16)
-    begin(mixes)
     lower, upper = turn(lower, ROWS), turn(upper, ROWS)
     inner = slice(DEEP, DEEP + ROWS)
     mix[inner, :LANES] = jnp.where(left, 0.0, lower).astype(BF16)
@@ -427,10 +425,10 @@
         jnp.sum(jnp.where(lanes_one == 2 * lon + c, cov[...], 0), axis=1, keepdims=True) > 0 for c in range(2)
     ]
 
-    def prepare(i, carry):
-        row = pl.multiple_of(i * 8, 8)
+    def prepare(i):
+        row = i * 8
         rows = pl.ds(row, 8)
-        inside = pl.ds(pl.multiple_of(BASE + row, 8), 8)
+        inside = pl.ds(BASE + row, 8)
         for c in range(2):
             cells = slice(c * LANES, (c + 1) * LANES)
             ext[U][c, inside, :] = vel[0, rows, cells]
@@ -454,12 +452,12 @@
                 ext[mass][c, inside, :] = 0.5 * open_mask / (volume + 1.0)
             for k in range(CATS):
                 thk_out[k, rows, cells] = thick[k]
-        return carry
-
-    lax.fori_loop(0, ROWS // 8, prepare, 0)
+
+    for i in range(ROWS // 8):
+        prepare(i)
 
     pack_sides(ext, rim_out, edge_out)
-    begin(halo)
+    begin(halo + mixes + sides)
     for pair, relay in zip(pairs, relays):
         pair.wait_recv()
         pl.when(passes_on)(relay.start)

time: 26.9 us -> 26.6 us (0.989)
  Pallas kernels: 26.1 us -> 25.8 us
    pallas_call x1, Pallas kernels: 25.2 us -> 24.9 us  [local(): pl.pallas_call(kernel, out_shape=[pltpu.VMEM(a.shape, F32) for a in (velo...]
where the time goes in v5:
time: 26.6 us; the launch traced here: 26.5 us
  Pallas kernels  25.8 us (97%)
  between operations  0.64 us (2%)
    pallas_call x1, Pallas kernels, local(): pl.pallas_call(kernel, out_shape=[pltpu.VMEM(a.shape, F32) for a in (velo...  24.9 us
    pallas_call x1, Pallas kernels, local(): pl.pallas_call(deliver, out_shape=[jax.ShapeDtypeStruct(a.shape, F32) for...  0.88 us

profile of v5, /device:TPU:1, one launch (start us, length us, event | category | flops | bytes accessed | tf_op | source)
XLA Modules:
  0.0 26.5 jit_solution(17676720020032703964)
XLA Ops:
  0.6 24.9 %shard_map.121 = (f32[2,64,256]{2,1,0:T(8,128)S(1)}, f32[3,64,256]{2,1,0:T(8,128)S(1)}, f32[6,64,256]{2,1,0:T(8,128)S(1)}) custom-call(f32[2,64,256]{2,1,0:T(8,128)} %vel_hbm.1, f32[3,64,256]{2,1,0:T(8,128)} %str_hbm.1, f32[6,64,256]{2,1,0:T(8,128)} %thk_hbm.1, f32[6,64,256]{2,1,0:T(8,128)} %con_hbm.1, s32[64,256]{1,0:T(8,128)} %land_hbm.1, ...), custom_call_target="tpu_custom_call" | custom-call | tf_op jit(solution)/shard_map/pallas_call | solution.py:548
  25.6 0.9 %shard_map.122 = (f32[2,64,256]{2,1,0:T(8,128)}, f32[3,64,256]{2,1,0:T(8,128)}, f32[6,64,256]{2,1,0:T(8,128)}) custom-call(f32[2,64,256]{2,1,0:T(8,128)S(1)} %get-tuple-element.6.vel, f32[3,64,256]{2,1,0:T(8,128)S(1)} %get-tuple-element.7.stress, f32[6,64,256]{2,1,0:T(8,128)S(1)} %get-tuple-element.8.thick), custom_call_target="tpu_custom_call" | custom-call | tf_op jit(solution)/shard_map/pallas_call | solution.py:570
